TPU v7x, 512 devices: a whole 4x4x16 slice. The times are simulated.
512 devices in a mesh: leaf: 64 (over y, z), samp: 8 (over x, core).
Axes of the slice: x: 4, y: 4, z: 16, core: 2. Of those that a mesh axis runs over, the one named last changes fastest.
Arguments:
- stiffness_block_row: bfloat16 [1024, 8, 128, 128], P('leaf'), may hold values from -2 to 2
- stored_block_column: int32 [1024, 8], P('leaf'), may hold values from 0 to 1023, as said below
- samples_t: bfloat16 [256, 131072], P('samp', 'leaf'), may hold values from -8 to 8
Outputs:
- products: float32 [256, 131072], P('samp', 'leaf')
- bases: float32 [256, 131072], P('samp', 'leaf')
- transfer_one: float32 [16384, 256], P('leaf', 'samp')
- transfer_two: float32 [16384, 256], P('leaf', 'samp')
- transfer_three: float32 [16384, 256], P('leaf', 'samp')
- top_factor: float32 [16384, 256], P('leaf', 'samp')
Inputs may be any that keep to these rules, and one draw needn't show every extreme that they name: `stored_block_column`: slot 0 of block row r names block column r; the other slots name block columns of the same leaf, or of a neighbouring leaf within 4 block rows of the boundary that the two leaves share; the first block row of every leaf that has a neighbour on a side reaches exactly 4 block rows into it, and every one of those 4 block rows is named by some block row of the leaf.
All inputs are finite; a program needn't handle non-finite values.
Results may differ from a plain program's by a relative error of at most 0.0003.
Values may be sent and summed in bfloat16 or wider, within the bound.
A program may use at most 64 MiB of HBM per device.

v0:
```python
import math

import jax
import jax.numpy as jnp
from jax import lax
from jax.sharding import PartitionSpec as P

HB = 4
LEVELS = 3


def with_halo(cells, sides, width):
    for axis, dim in sides:
        count = lax.axis_size(axis)
        ends = count - 1
        head = lax.slice_in_dim(cells, 0, width, axis=dim)
        tail = lax.slice_in_dim(cells, cells.shape[dim] - width, cells.shape[dim], axis=dim)
        cells = jnp.concatenate(
            [
                lax.ppermute(tail, axis, [(i, (i + 1) % count) for i in range(ends)]),
                cells,
                lax.ppermute(head, axis, [((i + 1) % count, i) for i in range(ends)]),
            ],
            axis=dim,
        )
    return cells


def from_partner(block, axis, bit):
    count = lax.axis_size(axis)
    route = []
    for low in range(count):
        high = low | 1 << bit
        if high != low and high < count:
            route += [(low, high), (high, low)]
    return lax.ppermute(block, axis, route)


def lower_solve(factor, right_side):
    return jax.scipy.linalg.solve_triangular(factor, right_side, lower=True)


def pick_blocks(sample_blocks, positions, keep_mask):
    sample_count = sample_blocks.shape[0]
    picked = jnp.take(sample_blocks, positions.reshape(-1), axis=1)
    picked = picked.reshape((sample_count,) + positions.shape + (sample_blocks.shape[2],))
    return jnp.where(keep_mask[None, :, :, None], picked, jnp.zeros_like(picked))


def shards(stiffness_block_row, stored_block_column, samples_t):
    block_sequence = stiffness_block_row.shape[2]
    blocks_here = stored_block_column.shape[0]
    sample_count = samples_t.shape[0]
    row_count = samples_t.shape[1]
    leaf_position_index = lax.axis_index("leaf")
    sample_index = lax.axis_index("samp")
    local_cols = stored_block_column - leaf_position_index * blocks_here
    inside = (local_cols >= 0) & (local_cols < blocks_here)
    own_blocks = samples_t.reshape(sample_count, blocks_here, block_sequence)
    near_terms = pick_blocks(own_blocks, jnp.clip(local_cols, 0, blocks_here - 1), inside)
    nearfield_portion = jnp.einsum(
        "rkij,srkj->sri", stiffness_block_row, near_terms, preferred_element_type=jnp.float32
    )
    window = with_halo(samples_t, (("leaf", 1),), HB * block_sequence)
    window_blocks = window.reshape(sample_count, blocks_here + 2 * HB, block_sequence)
    far_terms = pick_blocks(
        window_blocks,
        jnp.clip(local_cols + HB, 0, blocks_here + 2 * HB - 1),
        jnp.logical_not(inside),
    )
    far_part = jnp.einsum(
        "rkij,srkj->sri", stiffness_block_row, far_terms, preferred_element_type=jnp.float32
    )
    distant_portion = far_part.reshape(sample_count, row_count)
    products = (nearfield_portion + far_part).reshape(sample_count, row_count)
    gathered = lax.all_gather(distant_portion, "samp", axis=0, tiled=True)
    gramian_product = jnp.einsum("sr,tr->st", gathered, gathered, precision=lax.Precision.HIGHEST)

    def own_columns(matrix):
        return lax.dynamic_slice_in_dim(
            matrix, sample_index * sample_count, sample_count, matrix.ndim - 1
        )

    level_grams = [gramian_product]
    current = gramian_product
    for height in range(LEVELS):
        partner = from_partner(current, "leaf", height)
        current = current + partner
        level_grams.append(current)
    factors = jnp.linalg.cholesky(jnp.stack(level_grams))
    basis_whole = lower_solve(factors[0], gathered)
    leaf_basis = lax.dynamic_slice_in_dim(basis_whole, sample_index * sample_count, sample_count, 0)
    bases = leaf_basis * math.sqrt(row_count)
    child_pieces = own_columns(factors[:-1])
    transfer_blocks = jax.vmap(lower_solve)(factors[1:], child_pieces)
    top_factor = own_columns(factors[-1]) / math.sqrt(2**LEVELS * row_count)
    return (products, bases, transfer_blocks[0], transfer_blocks[1], transfer_blocks[2], top_factor)


def solution(mesh):
    return jax.shard_map(
        shards,
        mesh=mesh,
        in_specs=(P("leaf", None, None, None), P("leaf", None), P("samp", "leaf")),
        out_specs=(
            P("samp", "leaf"),
            P("samp", "leaf"),
            P("leaf", "samp"),
            P("leaf", "samp"),
            P("leaf", "samp"),
            P("leaf", "samp"),
        ),
        check_vma=False,
    )
```

profile of v0, /device:TPU:1, one launch (start us, length us, event | category | flops | bytes accessed | tf_op | source)
XLA Modules:
  0.0 362.7 jit_solution(11515370727346943241)
XLA Ops:
  7.2 0.8 fusion.45
  8.0 1.3 collective-permute-start.1
  9.3 5.0 %collective-permute-start = (bf16[32,512]{1,0:T(8,128)(2,1)S(1)}, bf16[32,512]{1,0:T(8,128)(2,1)S(1)}, u32[]{:S(2)}, u32[]{:S(2)}) collective-permute-start(bf16[32,512]{1,0:T(8,128)(2,1)S(1)} %get-tuple-element.83), channel_id=1, source_target_pairs={{0,8},{8,16},{16,24},{24,32},{32,40},{40,48},{48,56},{56,64},{64,7... | collective-permute-start | bytes 98312 | tf_op jit(solution)/shard_map/ppermute | solution.py:20
  14.3 0.7 compare_and_fusion
  15.4 0.9 copy_bitcast_fusion.2
  16.3 0.8 gather_fusion.1
  17.1 3.3 fusion.5
  20.4 0.7 copy_bitcast_fusion
  21.3 40.2 %all-gather.2.cloned.1.call-done = f32[256,2048]{1,0:T(8,128)} async-done(((f32[32,2048]{1,0:T(8,128)}), f32[256,2048]{1,0:T(8,128)}) %all-gather.2.cloned.1.call-update) | async-done | bytes 2097168 | tf_op jit(solution)/shard_map/all_gather | solution.py:76
  61.6 4.1 %fusion.46 = f32[256,256]{0,1:T(8,128)S(1)} fusion(f32[256,2048]{1,0:T(8,128)} %all-gather.2.cloned.1.call-done), kind=kOutput, calls=%fused_computation.101 | convolution fusion | flops 1610612736 | bytes 2359296 | tf_op jit(solution)/shard_map/sr,tr->st/dot_general | solution.py:77
  65.7 3.2 collective-permute-start.2
  68.9 6.2 %collective-permute-done.2 = f32[256,256]{0,1:T(8,128)S(1)} collective-permute-done((f32[256,256]{0,1:T(8,128)S(1)}, f32[256,256]{0,1:T(8,128)S(1)}, u32[]{:S(2)}, u32[]{:S(2)}) %collective-permute-start.2) | collective-permute-done | bytes 262176 | tf_op jit(solution)/shard_map/ppermute | solution.py:36
  75.2 4.2 %collective-permute-start.3 = (f32[256,256]{0,1:T(8,128)S(1)}, f32[256,256]{0,1:T(8,128)S(1)}, u32[]{:S(2)}, u32[]{:S(2)}) collective-permute-start(f32[256,256]{0,1:T(8,128)S(1)} %add.101), channel_id=1, source_target_pairs={{0,16},{16,0},{8,24},{24,8},{32,48},{48,32},{40,56},{56,40},{64,80... | collective-permute-start | bytes 786440 | tf_op jit(solution)/shard_map/ppermute | solution.py:36
  79.6 0.8 gather_fusion
  80.4 10.4 %collective-permute-done.3 = f32[256,256]{0,1:T(8,128)S(1)} collective-permute-done((f32[256,256]{0,1:T(8,128)S(1)}, f32[256,256]{0,1:T(8,128)S(1)}, u32[]{:S(2)}, u32[]{:S(2)}) %collective-permute-start.3) | collective-permute-done | bytes 262176 | tf_op jit(solution)/shard_map/ppermute | solution.py:36
  90.9 7.4 %collective-permute-start.4 = (f32[256,256]{0,1:T(8,128)S(1)}, f32[256,256]{0,1:T(8,128)S(1)}, u32[]{:S(2)}, u32[]{:S(2)}) collective-permute-start(f32[256,256]{0,1:T(8,128)S(1)} %add.102), channel_id=1, source_target_pairs={{0,32},{32,0},{8,40},{40,8},{16,48},{48,16},{24,56},{56,24},{64,96... | collective-permute-start | bytes 786440 | tf_op jit(solution)/shard_map/ppermute | solution.py:36
  98.2 3.4 fusion.1
  101.7 0.7 copy.156
  102.4 18.4 %collective-permute-done.4 = f32[256,256]{0,1:T(8,128)S(1)} collective-permute-done((f32[256,256]{0,1:T(8,128)S(1)}, f32[256,256]{0,1:T(8,128)S(1)}, u32[]{:S(2)}, u32[]{:S(2)}) %collective-permute-start.4) | collective-permute-done | bytes 262176 | tf_op jit(solution)/shard_map/ppermute | solution.py:36
  120.9 0.3 copy.120
  121.5 46.9 %custom-call.21 = f32[4,128,128]{2,1,0:T(8,128)S(1)} custom-call(f32[4,128,128]{2,1,0:T(8,128)S(1)} %cholesky.122), custom_call_target="Cholesky" | custom-call | tf_op jit(solution)/shard_map/jit(cholesky)/cholesky | solution.py:90
  168.5 39.3 %custom-call.22 = f32[4,1,128,128]{2,3,1,0:T(8,128)S(1)} custom-call(f32[4,1,128,128]{3,2,1,0:T(8,128)S(1)} %select_bitcast_fusion), custom_call_target="InvertDiagBlocksLowerTriangular" | custom-call | tf_op jit(solution)/shard_map/jit(cholesky)/cholesky | solution.py:90
  207.8 0.4 constant_dynamic-update-slice_fusion.1
  208.2 0.7 convolution_subtract_fusion.1
  208.9 46.9 %custom-call.23 = f32[4,128,128]{2,1,0:T(8,128)S(1)} custom-call(f32[4,128,128]{2,1,0:T(8,128)S(1)} %convolution_subtract_fusion.1), custom_call_target="Cholesky" | custom-call | tf_op jit(solution)/shard_map/jit(cholesky)/cholesky | solution.py:90
  256.2 1.3 slice_select_fusion
  257.7 5.2 %while.2 = (s32[]{:T(128)}, f32[256,256]{1,0:T(8,128)S(1)}, s32[2,2]{1,0:T(2,128)S(1)}, f32[2,128,128]{2,1,0:T(8,128)}, s32[]{:T(128)}) while((s32[]{:T(128)}, f32[256,256]{1,0:T(8,128)S(1)}, s32[2,2]{1,0:T(2,128)S(1)}, f32[2,128,128]{2,1,0:T(8,128)}, s32[]{:T(128)}) %tuple.57), condition=%wide.while_cond, body=%wide.while_body.sunk | while | flops 2 | bytes 132205 | solution.py:40
  257.7 0.6 fusion.61
  258.3 2.0 bitcast_dynamic-update-slice_fusion.4
  260.4 0.6 fusion.61
  260.9 2.0 bitcast_dynamic-update-slice_fusion.4
  263.0 20.5 %custom-call.24 = f32[2,128,128]{1,2,0:T(8,128)S(1)} custom-call(f32[2,128,128]{2,1,0:T(8,128)} %get-tuple-element.13), custom_call_target="InvertDiagBlocksLowerTriangular" | custom-call | tf_op jit(solution)/shard_map/jit(_solve_triangular)/triangular_solve | solution.py:40
  283.5 1.1 fusion.2
  284.5 1.0 convolution_subtract_fusion
  285.5 1.1 fusion.29
  286.7 5.4 %while.3 = (s32[]{:T(128)}, f32[3,256,256]{2,1,0:T(8,128)S(1)}, s32[2,2]{1,0:T(2,128)S(1)}, f32[2,3,128,128]{3,2,0,1:T(8,128)}, s32[]{:T(128)}) while((s32[]{:T(128)}, f32[3,256,256]{2,1,0:T(8,128)S(1)}, s32[2,2]{1,0:T(2,128)S(1)}, f32[2,3,128,128]{3,2,0,1:T(8,128)}, s32[]{:T(128)}) %tuple.66), condition=%wide.while_cond.1, body=%wide.while_body.1.sunk | while | flops 2 | bytes 394349 | solution.py:40
  286.7 0.6 fusion.62
  287.3 2.1 bitcast_dynamic-update-slice_fusion.5
  289.4 0.6 fusion.62
  290.0 2.1 bitcast_dynamic-update-slice_fusion.5
  292.1 59.8 %custom-call.25 = f32[3,2,128,128]{2,3,1,0:T(8,128)S(1)} custom-call(f32[3,2,128,128]{3,2,1,0:T(8,128)} %bitcast.128), custom_call_target="InvertDiagBlocksLowerTriangular" | custom-call | tf_op jit(solution)/shard_map/vmap(jit(_solve_triangular))/triangular_solve | solution.py:40
  351.9 0.8 fusion.19
  352.7 0.5 copy-done.3
  353.1 0.5 fusion.26
  353.7 0.3 convolution_subtract_fusion.2
  354.0 0.5 fusion.25
  354.4 0.6 fusion.34
  355.2 0.7 copy.132
  (53 shorter events, 2.1 us)
Async XLA Ops:
  7.2 54.4 %all-gather.2.cloned.1.call-start = ((), (), s32[]{:S(2)}) async-start(), calls=%async_computation | async-start | bytes 2359296 | tf_op jit(solution)/shard_map/all_gather | solution.py:76
  8.0 7.4 %collective-permute-start.1 = (bf16[32,512]{1,0:T(8,128)(2,1)S(1)}, bf16[32,512]{1,0:T(8,128)(2,1)S(1)}, u32[]{:S(2)}, u32[]{:S(2)}) collective-permute-start(bf16[32,512]{1,0:T(8,128)(2,1)S(1)} %get-tuple-element.84), channel_id=1, source_target_pairs={{8,0},{16,8},{24,16},{32,24},{40,32},{48,40},{56,48},{64,56},{72,6... | collective-permute-start | bytes 98312 | tf_op jit(solution)/shard_map/ppermute | solution.py:22
  9.3 6.1 %collective-permute-start = (bf16[32,512]{1,0:T(8,128)(2,1)S(1)}, bf16[32,512]{1,0:T(8,128)(2,1)S(1)}, u32[]{:S(2)}, u32[]{:S(2)}) collective-permute-start(bf16[32,512]{1,0:T(8,128)(2,1)S(1)} %get-tuple-element.83), channel_id=1, source_target_pairs={{0,8},{8,16},{16,24},{24,32},{32,40},{40,48},{48,56},{56,64},{64,7... | collective-permute-start | bytes 98312 | tf_op jit(solution)/shard_map/ppermute | solution.py:20
  21.3 47.5 %copy-start.4 = (bf16[32,2048]{1,0:T(8,128)(2,1)S(1)}, bf16[32,2048]{1,0:T(8,128)(2,1)}, u32[]{:S(2)}) copy-start(bf16[32,2048]{1,0:T(8,128)(2,1)} %param.5) | copy-start | bytes 393220
  65.7 9.5 %collective-permute-start.2 = (f32[256,256]{0,1:T(8,128)S(1)}, f32[256,256]{0,1:T(8,128)S(1)}, u32[]{:S(2)}, u32[]{:S(2)}) collective-permute-start(f32[256,256]{0,1:T(8,128)S(1)} %fusion.46), channel_id=1, source_target_pairs={{0,8},{8,0},{16,24},{24,16},{32,40},{40,32},{48,56},{56,48},{64,72... | collective-permute-start | bytes 786440 | tf_op jit(solution)/shard_map/ppermute | solution.py:36
  75.2 15.6 %collective-permute-start.3 = (f32[256,256]{0,1:T(8,128)S(1)}, f32[256,256]{0,1:T(8,128)S(1)}, u32[]{:S(2)}, u32[]{:S(2)}) collective-permute-start(f32[256,256]{0,1:T(8,128)S(1)} %add.101), channel_id=1, source_target_pairs={{0,16},{16,0},{8,24},{24,8},{32,48},{48,32},{40,56},{56,40},{64,80... | collective-permute-start | bytes 786440 | tf_op jit(solution)/shard_map/ppermute | solution.py:36
  90.9 30.0 %collective-permute-start.4 = (f32[256,256]{0,1:T(8,128)S(1)}, f32[256,256]{0,1:T(8,128)S(1)}, u32[]{:S(2)}, u32[]{:S(2)}) collective-permute-start(f32[256,256]{0,1:T(8,128)S(1)} %add.102), channel_id=1, source_target_pairs={{0,32},{32,0},{8,40},{40,8},{16,48},{48,16},{24,56},{56,24},{64,96... | collective-permute-start | bytes 786440 | tf_op jit(solution)/shard_map/ppermute | solution.py:36
  256.2 1.5 copy-start.1
  256.2 27.2 %copy-start = (f32[256,2048]{1,0:T(8,128)S(1)}, f32[256,2048]{1,0:T(8,128)}, u32[]{:S(2)}) copy-start(f32[256,2048]{1,0:T(8,128)} %all-gather.2.cloned.1.call-done) | copy-start | bytes 6291460
  285.5 1.1 copy-start.2
  292.1 63.0 %slice-start = ((f32[4,256,256]{2,1,0:T(8,128)}), f32[1,256,256]{2,1,0:T(8,128)S(1)}, s32[]{:S(2)}) async-start(f32[4,256,256]{2,1,0:T(8,128)} %copy-done.1), calls=%async_computation.1 | async-start | bytes 524288 | tf_op jit(solution)/shard_map/slice | solution.py:96
  351.9 1.2 copy-start.3
Sparse Core Ops, SparseCore 0:
  21.3 40.2 all-gather.1
where the time goes:
time: 363 us
  other arithmetic  219 us (60%)
  waiting for transfers between devices  75.3 us (21%)
  starting transfers between devices  21 us (6%)
  local copies, waits for them, and re-layouts  17 us (5%)
  matrix products  16.3 us (4%)
  between operations  14.4 us (4%)
    another operation x11, other arithmetic, shards(): factors = jnp.linalg.cholesky(jnp.stack(level_grams))  133 us
    another operation x6, other arithmetic, lower_solve(): return jax.scipy.linalg.solve_triangular(factor, right_side, lower=True)  81.6 us
    all_gather x1, waiting for transfers between devices, shards(): gathered = lax.all_gather(distant_portion, 'samp', axis=0, tiled=True)  40.2 us
    ppermute x3, waiting for transfers between devices, from_partner(): return lax.ppermute(block, axis, route)  35.1 us
    ppermute x3, starting transfers between devices, from_partner(): return lax.ppermute(block, axis, route)  14.7 us
    another operation x12, local copies, waits for them, and re-layouts  10.6 us
  transfers between devices with their start and end apart: 6, of which 4 were waited for; matrix products, arithmetic and copies ran while one was open for 2% of the time, Pallas kernels for 0%

commit v1 on v0

--- a/solution.py
+++ b/solution.py
@@ -1,8 +1,9 @@
-import math
-
-import jax
-import jax.numpy as jnp
+import functools, math
+import jax, jax.numpy as jnp
 from jax import lax
+from jax.experimental import pallas as pl
+from jax.experimental.pallas import tpu as pltpu
+
 from jax.sharding import PartitionSpec as P
 
 HB = 4
@@ -36,9 +37,97 @@
     return lax.ppermute(block, axis, route)
 
 
-def lower_solve(factor, right_side):
-    return jax.scipy.linalg.solve_triangular(factor, right_side, lower=True)
-
+HI = lax.Precision.HIGHEST
+RS = 136
+
+def dot_tn(a, b):
+    return lax.dot_general(a, b, (((0,), (0,)), ((), ())), precision=HI, preferred_element_type=jnp.float32)
+
+def dot_nt(a, b):
+    return lax.dot_general(a, b, (((1,), (1,)), ((), ())), precision=HI, preferred_element_type=jnp.float32)
+
+def dot_nn(a, b):
+    return lax.dot_general(a, b, (((1,), (0,)), ((), ())), precision=HI, preferred_element_type=jnp.float32)
+
+def lane(v, j):
+    return jnp.broadcast_to(v[:, j:j + 1], v.shape)
+
+def rows(i):
+    return pl.ds(i, 8, stride=RS)
+
+def panel8(x, y, r0):
+    a = [[lane(x[p], r0 + q) if q >= p else None for q in range(8)] for p in range(8)]
+    for p in range(8):
+        r = lax.rsqrt(a[p][p])
+        u = [a[p][q] * r if q > p else None for q in range(8)]
+        x[p] = x[p] * r
+        y[p] = y[p] * r
+        for s in range(p + 1, 8):
+            for q in range(s, 8):
+                a[s][q] = a[s][q] - u[s] * u[q]
+            x[s] = x[s] - u[s] * x[p]
+            y[s] = y[s] - u[s] * y[p]
+    return x, y
+
+def factor(X, Y, nb, sp=32):
+    for t in range(128 // sp):
+        base = t * sp
+        if t:
+            for b in range(nb):
+                lhs = X[b * RS:b * RS + base, base:base + sp]
+                rhs = jnp.concatenate([X[b * RS:b * RS + base, :], Y[b * RS:b * RS + base, :], Y[(4 + b) * RS:(4 + b) * RS + base, :]], axis=1)
+                up = dot_tn(lhs, rhs)
+                now = X[b * RS + base:b * RS + base + sp, :] - up[:, :128]
+                X[b * RS + base:b * RS + base + sp, :] = now
+                X[(4 + b) * RS + base:(4 + b) * RS + base + sp, :] = now
+                Y[b * RS + base:b * RS + base + sp, :] -= up[:, 128:256]
+                Y[(4 + b) * RS + base:(4 + b) * RS + base + sp, :] -= up[:, 256:]
+        xs = [X[rows(base + i), :] for i in range(sp)]
+        ys = [Y[rows(base + i), :] for i in range(sp)]
+        for g in range(sp // 8):
+            lo = g * 8
+            nx, ny = panel8(xs[lo:lo + 8], ys[lo:lo + 8], base + lo)
+            for p in range(8):
+                X[rows(base + lo + p), :] = nx[p]
+                Y[rows(base + lo + p), :] = ny[p]
+            for i in range(lo + 8, sp):
+                for p in range(8):
+                    m = lane(nx[p], base + i)
+                    xs[i] = xs[i] - m * nx[p]
+                    ys[i] = ys[i] - m * ny[p]
+
+def cholesky_inverse(G, U, W, X, Y, nb):
+    r = lax.broadcasted_iota(jnp.int32, (128, 128), 0)
+    c = lax.broadcasted_iota(jnp.int32, (128, 128), 1)
+    eye = (r == c).astype(jnp.float32)
+    up = c >= r
+    zero = jnp.zeros((128, 128), jnp.float32)
+    at = lambda g: slice(g * RS, g * RS + 128)
+    for b in range(nb):
+        X[at(b), :] = G[b, :128, :128]
+        X[at(4 + b), :] = G[b, :128, :128]
+        Y[at(b), :] = G[b, :128, 128:]
+        Y[at(4 + b), :] = eye
+    factor(X, Y, nb)
+    for b in range(nb):
+        u12 = Y[at(b), :]
+        w11 = Y[at(4 + b), :]
+        U[b, :128, :128] = jnp.where(up, X[at(b), :], zero)
+        U[b, :128, 128:] = u12
+        U[b, 128:, :128] = zero
+        W[b, :128, :128] = w11
+        W[b, :128, 128:] = zero
+        z = dot_tn(u12, jnp.concatenate([u12, w11], axis=1))
+        s = G[b, 128:, 128:] - z[:, :128]
+        X[at(b), :] = s
+        X[at(4 + b), :] = s
+        Y[at(b), :] = -z[:, 128:]
+        Y[at(4 + b), :] = eye
+    factor(X, Y, nb)
+    for b in range(nb):
+        U[b, 128:, 128:] = jnp.where(up, X[at(b), :], zero)
+        W[b, 128:, :128] = Y[at(b), :]
+        W[b, 128:, 128:] = Y[at(4 + b), :]
 
 def pick_blocks(sample_blocks, positions, keep_mask):
     sample_count = sample_blocks.shape[0]
@@ -76,25 +165,38 @@
     gathered = lax.all_gather(distant_portion, "samp", axis=0, tiled=True)
     gramian_product = jnp.einsum("sr,tr->st", gathered, gathered, precision=lax.Precision.HIGHEST)
 
-    def own_columns(matrix):
-        return lax.dynamic_slice_in_dim(
-            matrix, sample_index * sample_count, sample_count, matrix.ndim - 1
-        )
-
     level_grams = [gramian_product]
     current = gramian_product
     for height in range(LEVELS):
         partner = from_partner(current, "leaf", height)
         current = current + partner
         level_grams.append(current)
-    factors = jnp.linalg.cholesky(jnp.stack(level_grams))
-    basis_whole = lower_solve(factors[0], gathered)
-    leaf_basis = lax.dynamic_slice_in_dim(basis_whole, sample_index * sample_count, sample_count, 0)
-    bases = leaf_basis * math.sqrt(row_count)
-    child_pieces = own_columns(factors[:-1])
-    transfer_blocks = jax.vmap(lower_solve)(factors[1:], child_pieces)
-    top_factor = own_columns(factors[-1]) / math.sqrt(2**LEVELS * row_count)
-    return (products, bases, transfer_blocks[0], transfer_blocks[1], transfer_blocks[2], top_factor)
+    outs = finish(level_grams, gathered, sample_count)
+    return (products,) + tuple(outs)
+
+
+def finish_kernel(g0, g1, g2, g3, z, bases, one, two, three, top, G, U, W, X, Y):
+    for k, g in enumerate((g0, g1, g2, g3)):
+        G[k] = g[...]
+    cholesky_inverse(G, U, W, X, Y, 4)
+    count = bases.shape[0]
+    mine = pl.ds(pl.multiple_of(lax.axis_index("samp") * count, count), count)
+    bases[...] = dot_nn(W[0, mine, :], z[...]) * math.sqrt(z.shape[1])
+    for k, out in enumerate((one, two, three)):
+        out[...] = dot_nt(W[k + 1], U[k, mine, :])
+    top[...] = jnp.transpose(U[3, mine, :]) * (1.0 / math.sqrt(2**LEVELS * z.shape[1]))
+
+
+def finish(grams, gathered, count):
+    order, width = gathered.shape
+    f32 = jnp.float32
+    return pl.pallas_call(
+        finish_kernel,
+        out_shape=[jax.ShapeDtypeStruct((count, width), f32)] + [jax.ShapeDtypeStruct((order, count), f32)] * 4,
+        in_specs=[pl.BlockSpec(memory_space=pltpu.VMEM)] * 5,
+        out_specs=[pl.BlockSpec(memory_space=pltpu.VMEM)] * 5,
+        scratch_shapes=[pltpu.VMEM((4, order, order), f32)] * 3 + [pltpu.VMEM((8 * RS, 128), f32)] * 2,
+    )(*grams, gathered)
 
 
 def solution(mesh):

time: 363 us -> 152 us (0.42)
  other arithmetic: 219 us -> 2.48 us
  Pallas kernels: 0 us -> 16.8 us
  local copies, waits for them, and re-layouts: 17 us -> 10.8 us
  matrix products: 16.3 us -> 10.8 us
    another operation x17 -> x0, other arithmetic: 215 us -> none  [the longest x11 133 us: shards(): factors = jnp.linalg.cholesky(jnp.stack(level_grams))]
    pallas_call x0 -> x1, Pallas kernels: none -> 16.8 us  [finish(): pl.pallas_call(finish_kernel, out_shape=[jax.ShapeDtypeStruct((count, wid...]
    another operation x16 -> x0, local copies, waits for them, and re-layouts: 11.1 us -> none
    another operation x8 -> x0, matrix products: 5.48 us -> none  [the longest x6 4.43 us: lower_solve(): return jax.scipy.linalg.solve_triangular(factor, right_side, lower=True)]
    unnamed x11 -> x12, local copies, waits for them, and re-layouts: 1.4 us -> 6.39 us
  transfers between devices with their start and end apart: 6 -> 6, of which waited for: 4 -> 4; matrix products, arithmetic and copies ran while one was open for 2% -> 4% of each run, Pallas kernels for 0% -> 0%
where the time goes in v1:
time: 152 us
  waiting for transfers between devices  75.5 us (50%)
  starting transfers between devices  21 us (14%)
  Pallas kernels  16.8 us (11%)
  between operations  14.2 us (9%)
  local copies, waits for them, and re-layouts  10.8 us (7%)
  matrix products  10.8 us (7%)
  other arithmetic  2.48 us (2%)
    all_gather x1, waiting for transfers between devices, shards(): gathered = lax.all_gather(distant_portion, 'samp', axis=0, tiled=True)  40.5 us
    ppermute x3, waiting for transfers between devices, from_partner(): return lax.ppermute(block, axis, route)  35 us
    pallas_call x1, Pallas kernels, finish(): pl.pallas_call(finish_kernel, out_shape=[jax.ShapeDtypeStruct((count, wid...  16.8 us
    ppermute x3, starting transfers between devices, from_partner(): return lax.ppermute(block, axis, route)  14.7 us
    unnamed x12, local copies, waits for them, and re-layouts  6.39 us
    ppermute x1, starting transfers between devices, with_halo(): lax.ppermute(tail, axis, [(i, (i + 1) % count) for i in range(ends)])  4.99 us
    dot_general x1, matrix products, shards(): jnp.einsum('sr,tr->st', gathered, gathered, precision=lax.Precision.HIGHEST)  4.08 us
    dot_general x1, matrix products, shards(): jnp.einsum('rkij,srkj->sri', stiffness_block_row, near_terms, preferred_e...  3.42 us
  transfers between devices with their start and end apart: 6, of which 4 were waited for; matrix products, arithmetic and copies ran while one was open for 4% of the time, Pallas kernels for 0%

profile of v1, /device:TPU:1, one launch (start us, length us, event | category | flops | bytes accessed | tf_op | source)
XLA Modules:
  0.0 151.6 jit_solution(4456684152769037350)
XLA Ops:
  7.2 0.0 all-gather.2.cloned.1.call-start
  7.2 0.8 fusion.22
  8.0 1.3 collective-permute-start.1
  9.3 5.0 %collective-permute-start = (bf16[32,512]{1,0:T(8,128)(2,1)S(1)}, bf16[32,512]{1,0:T(8,128)(2,1)S(1)}, u32[]{:S(2)}, u32[]{:S(2)}) collective-permute-start(bf16[32,512]{1,0:T(8,128)(2,1)S(1)} %get-tuple-element.40), channel_id=1, source_target_pairs={{0,8},{8,16},{16,24},{24,32},{32,40},{40,48},{48,56},{56,64},{64,7... | collective-permute-start | bytes 98312 | tf_op jit(solution)/shard_map/ppermute | solution.py:21
  14.3 0.7 compare_and_fusion
  15.0 0.1 copy.40
  15.1 0.1 reshape.109
  15.2 0.1 copy.39
  15.3 0.1 copy.38
  15.3 0.0 collective-permute-done.1
  15.4 0.0 collective-permute-done
  15.4 0.9 copy_bitcast_fusion.2
  16.3 0.8 gather_fusion.1
  17.1 3.3 %fusion.2 = f32[16,32,128,1]{2,1,3,0:T(8,128)S(1)} fusion(bf16[16,8,128,128]{3,2,1,0:T(8,128)(2,1)} %param.3, bf16[32,16,8,128]{3,0,2,1:T(8,128)(2,1)S(1)} %bitcast.49, pred[16,8]{1,0:T(8,128)(4,1)S(1)} %copy.39, pred[16,8]{1,0:T(8,128)(4,1)S(1)} %copy.38), kind=kOutput, calls=%fused_computation.5 | convolution fusion | flops 135266304 | bytes 5505280 | tf_op jit(solution)/shard_map/rkij,srkj->sri/dot_general | solution.py:160
  20.4 0.0 copy-start.3
  20.4 0.7 copy_bitcast_fusion
  21.1 0.0 all-gather.2.cloned.1.call-update
  21.1 40.5 %all-gather.2.cloned.1.call-done.z = f32[256,2048]{1,0:T(8,128)} async-done(((f32[32,2048]{1,0:T(8,128)}), f32[256,2048]{1,0:T(8,128)}) %all-gather.2.cloned.1.call-update) | async-done | bytes 2097168 | tf_op jit(solution)/shard_map/all_gather | solution.py:165
  61.6 4.1 %fusion.23.g0 = f32[256,256]{1,0:T(8,128)S(1)} fusion(f32[256,2048]{1,0:T(8,128)} %all-gather.2.cloned.1.call-done.z), kind=kOutput, calls=%fused_computation.42 | convolution fusion | flops 1610612736 | bytes 2359296 | tf_op jit(solution)/shard_map/sr,tr->st/dot_general | solution.py:166
  65.7 0.0 copy-start
  65.7 3.2 %collective-permute-start.2 = (f32[256,256]{1,0:T(8,128)S(1)}, f32[256,256]{1,0:T(8,128)S(1)}, u32[]{:S(2)}, u32[]{:S(2)}) collective-permute-start(f32[256,256]{1,0:T(8,128)S(1)} %fusion.23.g0), channel_id=1, source_target_pairs={{0,8},{8,0},{16,24},{24,16},{32,40},{40,32},{48,56},{56,48},{64,72... | collective-permute-start | bytes 786440 | tf_op jit(solution)/shard_map/ppermute | solution.py:37
  68.9 0.1 copy.36
  69.0 0.1 reshape.107
  69.1 6.1 %collective-permute-done.2 = f32[256,256]{1,0:T(8,128)S(1)} collective-permute-done((f32[256,256]{1,0:T(8,128)S(1)}, f32[256,256]{1,0:T(8,128)S(1)}, u32[]{:S(2)}, u32[]{:S(2)}) %collective-permute-start.2) | collective-permute-done | bytes 262176 | tf_op jit(solution)/shard_map/ppermute | solution.py:37
  75.2 0.0 copy-start.1
  75.2 4.2 %collective-permute-start.3 = (f32[256,256]{1,0:T(8,128)S(1)}, f32[256,256]{1,0:T(8,128)S(1)}, u32[]{:S(2)}, u32[]{:S(2)}) collective-permute-start(f32[256,256]{1,0:T(8,128)S(1)} %add.70.g1), channel_id=1, source_target_pairs={{0,16},{16,0},{8,24},{24,8},{32,48},{48,32},{40,56},{56,40},{64,80... | collective-permute-start | bytes 786440 | tf_op jit(solution)/shard_map/ppermute | solution.py:37
  79.4 0.1 copy.35
  79.5 0.1 copy.34
  79.6 0.0 copy-done.3
  79.6 0.8 gather_fusion
  80.4 10.5 %collective-permute-done.3 = f32[256,256]{1,0:T(8,128)S(1)} collective-permute-done((f32[256,256]{1,0:T(8,128)S(1)}, f32[256,256]{1,0:T(8,128)S(1)}, u32[]{:S(2)}, u32[]{:S(2)}) %collective-permute-start.3) | collective-permute-done | bytes 262176 | tf_op jit(solution)/shard_map/ppermute | solution.py:37
  90.9 0.0 copy-start.2
  90.9 7.4 %collective-permute-start.4 = (f32[256,256]{1,0:T(8,128)S(1)}, f32[256,256]{1,0:T(8,128)S(1)}, u32[]{:S(2)}, u32[]{:S(2)}) collective-permute-start(f32[256,256]{1,0:T(8,128)S(1)} %add.71.g2), channel_id=1, source_target_pairs={{0,32},{32,0},{8,40},{40,8},{16,48},{48,16},{24,56},{56,24},{64,96... | collective-permute-start | bytes 786440 | tf_op jit(solution)/shard_map/ppermute | solution.py:37
  98.3 3.4 %fusion.1 = f32[16,4,8,128]{3,2,1,0:T(8,128)S(1)} fusion(bf16[16,8,128,128]{3,2,1,0:T(8,128)(2,1)} %param.3, bf16[32,16,8,128]{3,0,2,1:T(8,128)(2,1)S(1)} %bitcast.48, pred[16,8]{1,0:T(8,128)(4,1)S(1)} %copy.35, pred[16,8]{1,0:T(8,128)(4,1)S(1)} %copy.34, f32[16,32,128,1]{2,1,3,0:T(8,128)S(1)} %fusion.2), kind=kOutput, calls=%fused_computation.4 | convolution fusion | flops 135331840 | bytes 5767424 | tf_op jit(solution)/shard_map/rkij,srkj->sri/dot_general | solution.py:150
  101.7 0.0 copy-done
  101.7 0.0 copy-done.1
  101.7 0.7 copy.58
  102.4 18.4 %collective-permute-done.4 = f32[256,256]{1,0:T(8,128)S(1)} collective-permute-done((f32[256,256]{1,0:T(8,128)S(1)}, f32[256,256]{1,0:T(8,128)S(1)}, u32[]{:S(2)}, u32[]{:S(2)}) %collective-permute-start.4) | collective-permute-done | bytes 262176 | tf_op jit(solution)/shard_map/ppermute | solution.py:37
  120.9 0.8 add.72.g3
  121.6 0.0 copy-done.2
  121.6 16.8 %shard_map.82 = (f32[32,2048]{1,0:T(8,128)}, f32[256,32]{1,0:T(8,128)}, f32[256,32]{1,0:T(8,128)}, f32[256,32]{1,0:T(8,128)}, f32[256,32]{1,0:T(8,128)}) custom-call(f32[256,256]{1,0:T(8,128)} %copy-done, f32[256,256]{1,0:T(8,128)} %copy-done.1, f32[256,256]{1,0:T(8,128)} %copy-done.2, f32[256,256]{1,0:T(8,128)} %add.72.g3, ...), custom_call_target="tpu_custom_call" | custom-call | tf_op jit(solution)/shard_map/pallas_call | solution.py:193
  138.4 1.6 %copy.44 = f32[256,32]{0,1:T(8,128)} copy(f32[256,32]{1,0:T(8,128)} %get-tuple-element.30) | data formatting | bytes 65536
  140.0 1.6 %copy.45 = f32[256,32]{0,1:T(8,128)} copy(f32[256,32]{1,0:T(8,128)} %get-tuple-element.31) | data formatting | bytes 65536
  141.6 1.6 %copy.46 = f32[256,32]{0,1:T(8,128)} copy(f32[256,32]{1,0:T(8,128)} %get-tuple-element.32) | data formatting | bytes 65536
  143.2 1.6 %copy.47 = f32[256,32]{0,1:T(8,128)} copy(f32[256,32]{1,0:T(8,128)} %get-tuple-element.33) | data formatting | bytes 65536
  (7 shorter events, 0.1 us)
Async XLA Ops:
  7.2 54.4 %all-gather.2.cloned.1.call-start = ((), (), s32[]{:S(2)}) async-start(), calls=%async_computation | async-start | bytes 2359296 | tf_op jit(solution)/shard_map/all_gather | solution.py:165
  8.0 7.4 %collective-permute-start.1 = (bf16[32,512]{1,0:T(8,128)(2,1)S(1)}, bf16[32,512]{1,0:T(8,128)(2,1)S(1)}, u32[]{:S(2)}, u32[]{:S(2)}) collective-permute-start(bf16[32,512]{1,0:T(8,128)(2,1)S(1)} %get-tuple-element.41), channel_id=1, source_target_pairs={{8,0},{16,8},{24,16},{32,24},{40,32},{48,40},{56,48},{64,56},{72,6... | collective-permute-start | bytes 98312 | tf_op jit(solution)/shard_map/ppermute | solution.py:23
  9.3 6.1 %collective-permute-start = (bf16[32,512]{1,0:T(8,128)(2,1)S(1)}, bf16[32,512]{1,0:T(8,128)(2,1)S(1)}, u32[]{:S(2)}, u32[]{:S(2)}) collective-permute-start(bf16[32,512]{1,0:T(8,128)(2,1)S(1)} %get-tuple-element.40), channel_id=1, source_target_pairs={{0,8},{8,16},{16,24},{24,32},{32,40},{40,48},{48,56},{56,64},{64,7... | collective-permute-start | bytes 98312 | tf_op jit(solution)/shard_map/ppermute | solution.py:21
  20.4 59.2 %copy-start.3 = (bf16[32,2048]{1,0:T(8,128)(2,1)S(1)}, bf16[32,2048]{1,0:T(8,128)(2,1)}, u32[]{:S(2)}) copy-start(bf16[32,2048]{1,0:T(8,128)(2,1)} %param.5) | copy-start | bytes 393220
  65.7 36.0 %copy-start = (f32[256,256]{1,0:T(8,128)}, f32[256,256]{1,0:T(8,128)S(1)}, u32[]{:S(2)}) copy-start(f32[256,256]{1,0:T(8,128)S(1)} %fusion.23.g0) | copy-start | bytes 786436
  65.7 9.5 %collective-permute-start.2 = (f32[256,256]{1,0:T(8,128)S(1)}, f32[256,256]{1,0:T(8,128)S(1)}, u32[]{:S(2)}, u32[]{:S(2)}) collective-permute-start(f32[256,256]{1,0:T(8,128)S(1)} %fusion.23.g0), channel_id=1, source_target_pairs={{0,8},{8,0},{16,24},{24,16},{32,40},{40,32},{48,56},{56,48},{64,72... | collective-permute-start | bytes 786440 | tf_op jit(solution)/shard_map/ppermute | solution.py:37
  75.2 26.5 %copy-start.1 = (f32[256,256]{1,0:T(8,128)}, f32[256,256]{1,0:T(8,128)S(1)}, u32[]{:S(2)}) copy-start(f32[256,256]{1,0:T(8,128)S(1)} %add.70.g1) | copy-start | bytes 786436
  75.2 15.6 %collective-permute-start.3 = (f32[256,256]{1,0:T(8,128)S(1)}, f32[256,256]{1,0:T(8,128)S(1)}, u32[]{:S(2)}, u32[]{:S(2)}) collective-permute-start(f32[256,256]{1,0:T(8,128)S(1)} %add.70.g1), channel_id=1, source_target_pairs={{0,16},{16,0},{8,24},{24,8},{32,48},{48,32},{40,56},{56,40},{64,80... | collective-permute-start | bytes 786440 | tf_op jit(solution)/shard_map/ppermute | solution.py:37
  90.9 30.7 %copy-start.2 = (f32[256,256]{1,0:T(8,128)}, f32[256,256]{1,0:T(8,128)S(1)}, u32[]{:S(2)}) copy-start(f32[256,256]{1,0:T(8,128)S(1)} %add.71.g2) | copy-start | bytes 786436
  90.9 29.9 %collective-permute-start.4 = (f32[256,256]{1,0:T(8,128)S(1)}, f32[256,256]{1,0:T(8,128)S(1)}, u32[]{:S(2)}, u32[]{:S(2)}) collective-permute-start(f32[256,256]{1,0:T(8,128)S(1)} %add.71.g2), channel_id=1, source_target_pairs={{0,32},{32,0},{8,40},{40,8},{16,48},{48,16},{24,56},{56,24},{64,96... | collective-permute-start | bytes 786440 | tf_op jit(solution)/shard_map/ppermute | solution.py:37
Sparse Core Ops, SparseCore 0:
  21.3 40.2 all-gather.1

commit v2 on v1

v2 whole, which is shorter than its diff:
```python
import functools, math
import jax, jax.numpy as jnp
from jax import lax
from jax.experimental import pallas as pl
from jax.experimental.pallas import tpu as pltpu

from jax.sharding import PartitionSpec as P

HB = 4
NB = 8
LEVELS = 3
HOPS = (4, 5, 3, 6, 2, 7, 1, 0)
MESH = pl.DeviceIdType.MESH
HI = lax.Precision.HIGHEST
RS = 136

def dot_tn(a, b):
    return lax.dot_general(a, b, (((0,), (0,)), ((), ())), precision=HI, preferred_element_type=jnp.float32)

def dot_nt(a, b):
    return lax.dot_general(a, b, (((1,), (1,)), ((), ())), precision=HI, preferred_element_type=jnp.float32)

def dot_nt_fast(a, b):
    return lax.dot_general(a, b, (((1,), (1,)), ((), ())), preferred_element_type=jnp.float32)

def dot_nn(a, b):
    return lax.dot_general(a, b, (((1,), (0,)), ((), ())), precision=HI, preferred_element_type=jnp.float32)

def lane(v, j):
    return jnp.broadcast_to(v[:, j:j + 1], v.shape)

def rows(i):
    return pl.ds(i, 8, stride=RS)

def panel8(x, y, r0):
    a = [[lane(x[p], r0 + q) if q >= p else None for q in range(8)] for p in range(8)]
    for p in range(8):
        r = lax.rsqrt(a[p][p])
        u = [a[p][q] * r if q > p else None for q in range(8)]
        x[p] = x[p] * r
        y[p] = y[p] * r
        for s in range(p + 1, 8):
            for q in range(s, 8):
                a[s][q] = a[s][q] - u[s] * u[q]
            x[s] = x[s] - u[s] * x[p]
            y[s] = y[s] - u[s] * y[p]
    return x, y

def factor(X, Y, nb, sp=32):
    for t in range(128 // sp):
        base = t * sp
        if t:
            for b in range(nb):
                lhs = X[b * RS:b * RS + base, base:base + sp]
                rhs = jnp.concatenate([X[b * RS:b * RS + base, :], Y[b * RS:b * RS + base, :], Y[(4 + b) * RS:(4 + b) * RS + base, :]], axis=1)
                up = dot_tn(lhs, rhs)
                now = X[b * RS + base:b * RS + base + sp, :] - up[:, :128]
                X[b * RS + base:b * RS + base + sp, :] = now
                X[(4 + b) * RS + base:(4 + b) * RS + base + sp, :] = now
                Y[b * RS + base:b * RS + base + sp, :] -= up[:, 128:256]
                Y[(4 + b) * RS + base:(4 + b) * RS + base + sp, :] -= up[:, 256:]
        xs = [X[rows(base + i), :] for i in range(sp)]
        ys = [Y[rows(base + i), :] for i in range(sp)]
        for g in range(sp // 8):
            lo = g * 8
            nx, ny = panel8(xs[lo:lo + 8], ys[lo:lo + 8], base + lo)
            for p in range(8):
                X[rows(base + lo + p), :] = nx[p]
                Y[rows(base + lo + p), :] = ny[p]
            for i in range(lo + 8, sp):
                for p in range(8):
                    m = lane(nx[p], base + i)
                    xs[i] = xs[i] - m * nx[p]
                    ys[i] = ys[i] - m * ny[p]

def cholesky_inverse(G, U, W, X, Y, nb):
    r = lax.broadcasted_iota(jnp.int32, (128, 128), 0)
    c = lax.broadcasted_iota(jnp.int32, (128, 128), 1)
    eye = (r == c).astype(jnp.float32)
    up = c >= r
    zero = jnp.zeros((128, 128), jnp.float32)
    at = lambda g: slice(g * RS, g * RS + 128)
    for b in range(nb):
        X[at(b), :] = G(b, 0)
        X[at(4 + b), :] = G(b, 0)
        Y[at(b), :] = G(b, 1)
        Y[at(4 + b), :] = eye
    factor(X, Y, nb)
    for b in range(nb):
        u12 = Y[at(b), :]
        w11 = Y[at(4 + b), :]
        U[b, :128, :128] = jnp.where(up, X[at(b), :], zero)
        U[b, :128, 128:] = u12
        U[b, 128:, :128] = zero
        W[b, :128, :128] = w11
        W[b, :128, 128:] = zero
        z = dot_tn(u12, jnp.concatenate([u12, w11], axis=1))
        s = G(b, 2) - z[:, :128]
        X[at(b), :] = s
        X[at(4 + b), :] = s
        Y[at(b), :] = -z[:, 128:]
        Y[at(4 + b), :] = eye
    factor(X, Y, nb)
    for b in range(nb):
        U[b, 128:, 128:] = jnp.where(up, X[at(b), :], zero)
        W[b, 128:, :128] = Y[at(b), :]
        W[b, 128:, 128:] = Y[at(4 + b), :]

def greet(barrier, there, sample):
    pl.semaphore_signal(barrier, inc=1, device_id=(there, sample), device_id_type=MESH)


def window_kernel(leaves, own, win, halo_send, halo_recv):
    leaf = lax.axis_index("leaf")
    me = lax.axis_index("samp")
    group = lax.axis_size("samp")
    count = own.shape[0]
    width = HB * 128
    barrier = pltpu.get_barrier_semaphore()
    for hop in HOPS:
        peer = lax.rem(me + hop, group)
        @pl.when(leaf > 0)
        def _():
            greet(barrier, leaf - 1, peer)
        @pl.when(leaf < leaves - 1)
        def _():
            greet(barrier, leaf + 1, peer)
    @pl.when(leaf == 0)
    def _():
        win[:, :width] = jnp.zeros((win.shape[0], width), win.dtype)
    @pl.when(leaf == leaves - 1)
    def _():
        win[:, width:] = jnp.zeros((win.shape[0], width), win.dtype)
    neighbours = jnp.minimum(leaf, 1) + jnp.minimum(leaves - 1 - leaf, 1)
    pl.semaphore_wait(barrier, group * neighbours)

    def halo(side, sample_from, sample_to, hop):
        start = (own.shape[1] - width) * (1 - side)
        at = pl.ds(pl.multiple_of(sample_from * count, count), count)
        return pltpu.make_async_remote_copy(
            src_ref=own.at[:, pl.ds(start, width)],
            dst_ref=win.at[at, pl.ds(side * width, width)],
            send_sem=halo_send.at[side, hop],
            recv_sem=halo_recv.at[side, sample_from],
            device_id=(leaf + 1 - 2 * side, sample_to),
            device_id_type=MESH,
        )

    for hop in HOPS:
        peer = lax.rem(me + hop, group)
        @pl.when(leaf < leaves - 1)
        def _():
            halo(0, me, peer, hop).start()
        @pl.when(leaf > 0)
        def _():
            halo(1, me, peer, hop).start()
    for hop in HOPS:
        peer = lax.rem(me + hop, group)
        @pl.when(leaf > 0)
        def _():
            halo(0, peer, me, hop).wait_recv()
        @pl.when(leaf < leaves - 1)
        def _():
            halo(1, peer, me, hop).wait_recv()
    for hop in HOPS:
        peer = lax.rem(me + hop, group)
        @pl.when(leaf < leaves - 1)
        def _():
            halo(0, me, peer, hop).wait_send()
        @pl.when(leaf > 0)
        def _():
            halo(1, me, peer, hop).wait_send()


def window(leaves, samples_t):
    count = samples_t.shape[0]
    group = 8
    vmem = pl.BlockSpec(memory_space=pltpu.VMEM)
    return pl.pallas_call(
        functools.partial(window_kernel, leaves),
        out_shape=jax.ShapeDtypeStruct((group * count, 2 * HB * 128), samples_t.dtype),
        in_specs=[vmem],
        out_specs=vmem,
        scratch_shapes=[pltpu.SemaphoreType.DMA((2, group))] * 2,
        compiler_params=pltpu.CompilerParams(collective_id=0, has_side_effects=True),
        cost_estimate=pl.CostEstimate(flops=0, bytes_accessed=1 << 20, transcendentals=0),
    )(samples_t)


def block_row(A, picks, r):
    blocks = [A[r, k] for k in range(NB)]
    return dot_nt_fast(jnp.concatenate(picks, axis=1), jnp.concatenate(blocks, axis=1))


def product_kernel(cols, A, own, win, z, products, gram):
    leaf = lax.axis_index("leaf")
    count = own.shape[0]
    depth = cols.shape[0]
    mine = pl.ds(pl.multiple_of(lax.axis_index("samp") * count, count), count)

    def one_row(r):
        far, near = [], []
        for k in range(NB):
            local = cols[r, k] - leaf * depth
            inside = (local >= 0) & (local < depth)
            place = jnp.clip(jnp.where(local < 0, local + HB, local - depth + HB), 0, 2 * HB - 1)
            pick = win[:, pl.ds(pl.multiple_of(place * 128, 128), 128)]
            far.append(jnp.where(inside, jnp.zeros_like(pick), pick))
            pick = own[:, pl.ds(pl.multiple_of(jnp.clip(local, 0, depth - 1) * 128, 128), 128)]
            near.append(jnp.where(inside, pick, jnp.zeros_like(pick)))
        both = [jnp.concatenate([f, n], axis=0) for f, n in zip(far, near)]
        out = block_row(A, both, r)
        return out[:-count], out[-count:]

    gram[...] = jnp.zeros_like(gram)

    def step(q, carry):
        parts = [one_row(2 * q + i) for i in range(2)]
        pair = jnp.concatenate([p[0] for p in parts], axis=1)
        here = pl.ds(pl.multiple_of(q * 256, 256), 256)
        z[:, here] = pair
        products[:, here] = jnp.concatenate([p[1] for p in parts], axis=1)
        upper = dot_nt(pair[:128], pair)
        gram[0] += upper[:, :128]
        gram[1] += upper[:, 128:]
        gram[2] += dot_nt(pair[128:], pair[128:])
        return carry

    lax.fori_loop(0, depth // 2, step, 0)
    products[...] += z[mine, :]


def product(stiffness_block_row, stored_block_column, samples_t, win):
    f32 = jnp.float32
    count, width = samples_t.shape
    vmem = pl.BlockSpec(memory_space=pltpu.VMEM)
    return pl.pallas_call(
        product_kernel,
        out_shape=[
            jax.ShapeDtypeStruct((win.shape[0], width), f32),
            jax.ShapeDtypeStruct((count, width), f32),
            jax.ShapeDtypeStruct((3, 128, 128), f32),
        ],
        in_specs=[pl.BlockSpec(memory_space=pltpu.SMEM), vmem, vmem, vmem],
        out_specs=[vmem] * 3,
        cost_estimate=pl.CostEstimate(flops=10**10, bytes_accessed=8 << 20, transcendentals=0),
    )(stored_block_column, stiffness_block_row, samples_t, win)


def levels_kernel(gram, levels, part, got, pair_send, pair_recv, all_send, all_recv):
    leaf = lax.axis_index("leaf")
    me = lax.axis_index("samp")
    group = lax.axis_size("samp")
    barrier = pltpu.get_barrier_semaphore()
    partners = [leaf + (1 << h) - 2 * (1 << h) * lax.rem(leaf // (1 << h), 2) for h in range(LEVELS)]
    for h in reversed(range(LEVELS)):
        greet(barrier, partners[h], me)
    for hop in HOPS[:-1]:
        greet(barrier, leaf, lax.rem(me + hop, group))
    slab = 128 // group
    rows_here = pl.ds(pl.multiple_of(me * slab, slab), slab)
    for j in range(3):
        part[0, j * slab:(j + 1) * slab, :] = gram[j, rows_here, :]
    pl.semaphore_wait(barrier, group - 1 + LEVELS)

    def trade(h):
        return pltpu.make_async_remote_copy(
            src_ref=part.at[h], dst_ref=got.at[h], send_sem=pair_send.at[h], recv_sem=pair_recv.at[h],
            device_id=(partners[h], me), device_id_type=MESH,
        )

    def share(h, sample_from, sample_to, hop):
        return pltpu.make_async_remote_copy(
            src_ref=part.at[h + 1], dst_ref=levels.at[h, sample_from],
            send_sem=all_send.at[h, hop], recv_sem=all_recv.at[h, sample_from],
            device_id=(leaf, sample_to), device_id_type=MESH,
        )

    trade(0).start()
    for h in range(LEVELS):
        trade(h).wait_recv()
        total = part[h] + got[h]
        part[h + 1] = total
        if h + 1 < LEVELS:
            trade(h + 1).start()
        for hop in HOPS[:-1]:
            share(h, me, lax.rem(me + hop, group), hop).start()
        levels[h, me] = total
    for h in range(LEVELS):
        for hop in HOPS[:-1]:
            share(h, lax.rem(me + hop, group), me, hop).wait_recv()
    for h in range(LEVELS):
        trade(h).wait_send()
        for hop in HOPS[:-1]:
            share(h, me, lax.rem(me + hop, group), hop).wait_send()


def exchange(gram):
    f32 = jnp.float32
    group = 8
    slab = 128 // group
    vmem = pl.BlockSpec(memory_space=pltpu.VMEM)
    return pl.pallas_call(
        levels_kernel,
        out_shape=jax.ShapeDtypeStruct((LEVELS, group, 3 * slab, 128), f32),
        in_specs=[vmem],
        out_specs=vmem,
        scratch_shapes=[
            pltpu.VMEM((LEVELS + 1, 3 * slab, 128), f32),
            pltpu.VMEM((LEVELS, 3 * slab, 128), f32),
            pltpu.SemaphoreType.DMA((LEVELS,)),
            pltpu.SemaphoreType.DMA((LEVELS,)),
            pltpu.SemaphoreType.DMA((LEVELS, group)),
            pltpu.SemaphoreType.DMA((LEVELS, group)),
        ],
        compiler_params=pltpu.CompilerParams(collective_id=1, has_side_effects=True),
        cost_estimate=pl.CostEstimate(flops=0, bytes_accessed=1 << 20, transcendentals=0),
    )(gram)


def finish_kernel(g0, lv, z, bases, one, two, three, top, U, W, X, Y):
    count, width = bases.shape
    slab = lv.shape[2] // 3
    def block(b, j):
        if b == 0:
            return g0[j]
        return jnp.concatenate([lv[b - 1, s, j * slab:(j + 1) * slab, :] for s in range(lv.shape[1])], axis=0)
    cholesky_inverse(block, U, W, X, Y, 4)
    mine = pl.ds(pl.multiple_of(lax.axis_index("samp") * count, count), count)
    bases[...] = dot_nn(W[0, mine, :], z[...]) * math.sqrt(width)
    for k, out in enumerate((one, two, three)):
        out[...] = dot_nt(W[k + 1], U[k, mine, :])
    top[...] = jnp.transpose(U[3, mine, :]) * (1.0 / math.sqrt(2**LEVELS * width))


def finish(gram, levels, z, count):
    order, width = z.shape
    f32 = jnp.float32
    vmem = pl.BlockSpec(memory_space=pltpu.VMEM)
    return pl.pallas_call(
        finish_kernel,
        out_shape=[jax.ShapeDtypeStruct((count, width), f32)] + [jax.ShapeDtypeStruct((order, count), f32)] * 4,
        in_specs=[vmem] * 3,
        out_specs=[vmem] * 5,
        scratch_shapes=[pltpu.VMEM((4, order, order), f32)] * 2 + [pltpu.VMEM((8 * RS, 128), f32)] * 2,
        cost_estimate=pl.CostEstimate(flops=10**10, bytes_accessed=4 << 20, transcendentals=0),
    )(gram, levels, z)


def shards(leaves, stiffness_block_row, stored_block_column, samples_t):
    win = window(leaves, samples_t)
    z, products, gram = product(stiffness_block_row, stored_block_column, samples_t, win)
    levels = exchange(gram)
    return (products,) + tuple(finish(gram, levels, z, samples_t.shape[0]))


def solution(mesh):
    return jax.shard_map(
        functools.partial(shards, mesh.shape["leaf"]),
        mesh=mesh,
        in_specs=(P("leaf", None, None, None), P("leaf", None), P("samp", "leaf")),
        out_specs=(
            P("samp", "leaf"),
            P("samp", "leaf"),
            P("leaf", "samp"),
            P("leaf", "samp"),
            P("leaf", "samp"),
            P("leaf", "samp"),
        ),
        check_vma=False,
    )
```

time: 152 us -> 81.4 us (0.54)
  waiting for transfers between devices: 75.5 us -> 0 us
  Pallas kernels: 16.8 us -> 72.7 us
  starting transfers between devices: 21 us -> 0 us
  between operations: 14.2 us -> 0.65 us
  matrix products: 10.8 us -> 0 us
  local copies, waits for them, and re-layouts: 10.8 us -> 7.73 us
  other arithmetic: 2.48 us -> 0 us
    pallas_call x0 -> x3, Pallas kernels: none -> 56 us  [the longest x1 26.3 us: exchange(): pl.pallas_call(levels_kernel, out_shape=jax.ShapeDtypeStruct((LEVELS, gro...]
    all_gather x1 -> x0, waiting for transfers between devices: 40.5 us -> none  [shards(): gathered = lax.all_gather(distant_portion, 'samp', axis=0, tiled=True)]
    ppermute x5 -> x0, waiting for transfers between devices: 35 us -> none  [the longest x3 35 us: from_partner(): return lax.ppermute(block, axis, route)]
    ppermute x5 -> x0, starting transfers between devices: 21 us -> none  [the longest x3 14.7 us: from_partner(): return lax.ppermute(block, axis, route)]
    dot_general x3 -> x0, matrix products: 10.8 us -> none  [the longest x1 4.08 us: shards(): jnp.einsum('sr,tr->st', gathered, gathered, precision=lax.Precision.HIGHEST)]
    reshape x5 -> x0, local copies, waits for them, and re-layouts: 1.66 us -> none  [the longest x1 0.74 us: shards(): distant_portion = far_part.reshape(sample_count, row_count)]
    gather x2 -> x0, local copies, waits for them, and re-layouts: 1.53 us -> none  [pick_blocks(): picked = jnp.take(sample_blocks, positions.reshape(-1), axis=1)]
    unnamed x12 -> x5, local copies, waits for them, and re-layouts: 6.39 us -> 7.73 us
  transfers between devices with their start and end apart: 6 -> 0, of which waited for: 4 -> 0; matrix products, arithmetic and copies ran while one was open for 4% -> 0% of each run, Pallas kernels for 0% -> 0%
where the time goes in v2:
time: 81.4 us; the launch traced here: 81.1 us
  Pallas kernels  72.7 us (89%)
  local copies, waits for them, and re-layouts  7.73 us (9%)
    pallas_call x1, Pallas kernels, exchange(): pl.pallas_call(levels_kernel, out_shape=jax.ShapeDtypeStruct((LEVELS, gro...  26.3 us
    pallas_call x1, Pallas kernels, window(): pl.pallas_call(functools.partial(window_kernel, leaves), out_shape=jax.Sh...  17.8 us
    pallas_call x1, Pallas kernels, finish(): pl.pallas_call(finish_kernel, out_shape=[jax.ShapeDtypeStruct((count, wid...  16.7 us
    pallas_call x1, Pallas kernels, product(): pl.pallas_call(product_kernel, out_shape=[jax.ShapeDtypeStruct((win.shape...  11.9 us
    unnamed x5, local copies, waits for them, and re-layouts  7.73 us

profile of v2, /device:TPU:1, one launch (start us, length us, event | category | flops | bytes accessed | tf_op | source)
XLA Modules:
  0.0 81.1 jit_solution(61328796314405846)
XLA Ops:
  0.6 1.4 %copy.9.cols = s32[16,8]{1,0:T(8,128)} copy(s32[16,8]{0,1:T(8,128)} %param.4) | data formatting | bytes 1024 | tf_op args[1]
  2.0 17.8 %shard_map.82.win = bf16[256,1024]{1,0:T(8,128)(2,1)} custom-call(bf16[32,2048]{1,0:T(8,128)(2,1)} %own.3), custom_call_target="tpu_custom_call" | custom-call | bytes 1048576 | tf_op jit(solution)/shard_map/pallas_call | solution.py:179
  19.8 11.9 %shard_map.83 = (f32[256,2048]{1,0:T(8,128)}, f32[32,2048]{1,0:T(8,128)}, f32[3,128,128]{2,1,0:T(8,128)}) custom-call(s32[16,8]{1,0:T(8,128)} %copy.9.cols, bf16[16,8,128,128]{3,2,1,0:T(8,128)(2,1)} %A.1, bf16[32,2048]{1,0:T(8,128)(2,1)} %own.3, bf16[256,1024]{1,0:T(8,128)(2,1)} %shard_map.82.win), custom_call_target="tpu_custom_call" | custom-call | flops 10000000000 | bytes 8388608 | tf_op jit(solution)/shard_map/pallas_call | solution.py:237
  31.7 26.3 %shard_map.84.lv = f32[3,8,48,128]{3,2,1,0:T(8,128)} custom-call(f32[3,128,128]{2,1,0:T(8,128)} %get-tuple-element.15.gram.g0), custom_call_target="tpu_custom_call" | custom-call | bytes 1048576 | tf_op jit(solution)/shard_map/pallas_call | solution.py:303
  58.0 16.7 %shard_map.85 = (f32[32,2048]{1,0:T(8,128)}, f32[256,32]{1,0:T(8,128)}, f32[256,32]{1,0:T(8,128)}, f32[256,32]{1,0:T(8,128)}, f32[256,32]{1,0:T(8,128)}) custom-call(f32[3,128,128]{2,1,0:T(8,128)} %get-tuple-element.15.gram.g0, f32[3,8,48,128]{3,2,1,0:T(8,128)} %shard_map.84.lv, f32[256,2048]{1,0:T(8,128)} %get-tuple-element.16.z), custom_call_target="tpu_custom_call" | custom-call | flops 10000000000 | bytes 4194304 | tf_op jit(solution)/shard_map/pallas_call | solution.py:340
  74.7 1.6 %copy.10 = f32[256,32]{0,1:T(8,128)} copy(f32[256,32]{1,0:T(8,128)} %get-tuple-element.24) | data formatting | bytes 65536
  76.3 1.6 %copy.11 = f32[256,32]{0,1:T(8,128)} copy(f32[256,32]{1,0:T(8,128)} %get-tuple-element.25) | data formatting | bytes 65536
  77.9 1.6 %copy.12 = f32[256,32]{0,1:T(8,128)} copy(f32[256,32]{1,0:T(8,128)} %get-tuple-element.26) | data formatting | bytes 65536
  79.5 1.6 %copy.13 = f32[256,32]{0,1:T(8,128)} copy(f32[256,32]{1,0:T(8,128)} %get-tuple-element.27) | data formatting | bytes 65536

commit v3 on v2

--- a/solution.py
+++ b/solution.py
@@ -110,21 +110,26 @@
     pl.semaphore_signal(barrier, inc=1, device_id=(there, sample), device_id_type=MESH)
 
 
-def window_kernel(leaves, own, win, halo_send, halo_recv):
+def window_kernel(leaves, own, win, halo_send, east_send, west_send, mate_send, recv):
     leaf = lax.axis_index("leaf")
     me = lax.axis_index("samp")
     group = lax.axis_size("samp")
+    chips = group // 2
+    chip, core = me // 2, lax.rem(me, 2)
     count = own.shape[0]
     width = HB * 128
+    east = 2 * lax.rem(chip + 1, chips) + core
+    west = 2 * lax.rem(chip + chips - 1, chips) + core
+    mate = 2 * chip + 1 - core
     barrier = pltpu.get_barrier_semaphore()
-    for hop in HOPS:
-        peer = lax.rem(me + hop, group)
-        @pl.when(leaf > 0)
-        def _():
-            greet(barrier, leaf - 1, peer)
-        @pl.when(leaf < leaves - 1)
-        def _():
-            greet(barrier, leaf + 1, peer)
+    @pl.when(leaf > 0)
+    def _():
+        greet(barrier, leaf - 1, me)
+    @pl.when(leaf < leaves - 1)
+    def _():
+        greet(barrier, leaf + 1, me)
+    for peer in (east, west, mate):
+        greet(barrier, leaf, peer)
     @pl.when(leaf == 0)
     def _():
         win[:, :width] = jnp.zeros((win.shape[0], width), win.dtype)
@@ -132,44 +137,101 @@
     def _():
         win[:, width:] = jnp.zeros((win.shape[0], width), win.dtype)
     neighbours = jnp.minimum(leaf, 1) + jnp.minimum(leaves - 1 - leaf, 1)
-    pl.semaphore_wait(barrier, group * neighbours)
-
-    def halo(side, sample_from, sample_to, hop):
-        start = (own.shape[1] - width) * (1 - side)
-        at = pl.ds(pl.multiple_of(sample_from * count, count), count)
+    pl.semaphore_wait(barrier, 3 + neighbours)
+
+    def place(side, sample):
+        return win.at[pl.ds(pl.multiple_of(sample * count, count), count), pl.ds(side * width, width)]
+
+    def send(source, side, sample, send_sem, slot, there, to):
         return pltpu.make_async_remote_copy(
-            src_ref=own.at[:, pl.ds(start, width)],
-            dst_ref=win.at[at, pl.ds(side * width, width)],
-            send_sem=halo_send.at[side, hop],
-            recv_sem=halo_recv.at[side, sample_from],
-            device_id=(leaf + 1 - 2 * side, sample_to),
-            device_id_type=MESH,
+            src_ref=source, dst_ref=place(side, sample), send_sem=send_sem, recv_sem=recv.at[side, slot[0], slot[1]],
+            device_id=(there, to), device_id_type=MESH,
         )
 
-    for hop in HOPS:
-        peer = lax.rem(me + hop, group)
-        @pl.when(leaf < leaves - 1)
+    def halo(side):
+        tail = own.at[:, pl.ds((own.shape[1] - width) * (1 - side), width)]
+        return send(tail, side, me, halo_send.at[side], (0, 0), leaf + 1 - 2 * side, me)
+
+    def origin(away):
+        return 2 * lax.rem(chip + away, chips) + core
+
+    def to_east(side, away):
+        return send(place(side, origin(away)), side, origin(away), east_send.at[side, away // 3],
+                    ((away + chips - 1) % chips, 0), leaf, east)
+
+    def to_west(side, away):
+        return send(place(side, origin(away)), side, origin(away), west_send.at[side, away],
+                    (away + 1, 0), leaf, west)
+
+    def to_mate(side, away):
+        return send(place(side, origin(away)), side, origin(away), mate_send.at[side, away], (away, 1), leaf, mate)
+
+    def arrived(side, away, other):
+        sample = 2 * lax.rem(chip + away, chips) + (1 - core if other else core)
+        send(place(side, sample), side, sample, mate_send.at[side, away], (away, other), leaf, mate).wait_recv()
+
+    def if_side(side, do):
+        @pl.when((leaf < leaves - 1) if side else (leaf > 0))
         def _():
-            halo(0, me, peer, hop).start()
-        @pl.when(leaf > 0)
-        def _():
-            halo(1, me, peer, hop).start()
-    for hop in HOPS:
-        peer = lax.rem(me + hop, group)
-        @pl.when(leaf > 0)
-        def _():
-            halo(0, peer, me, hop).wait_recv()
-        @pl.when(leaf < leaves - 1)
-        def _():
-            halo(1, peer, me, hop).wait_recv()
-    for hop in HOPS:
-        peer = lax.rem(me + hop, group)
-        @pl.when(leaf < leaves - 1)
-        def _():
-            halo(0, me, peer, hop).wait_send()
-        @pl.when(leaf > 0)
-        def _():
-            halo(1, me, peer, hop).wait_send()
+            do()
+
+    @pl.when(leaf < leaves - 1)
+    def _():
+        halo(0).start()
+    @pl.when(leaf > 0)
+    def _():
+        halo(1).start()
+
+    def own_rows(side):
+        def do():
+            arrived(side, 0, 0)
+            to_east(side, 0).start()
+            to_west(side, 0).start()
+            to_mate(side, 0).start()
+        return do
+
+    def onward(side):
+        def do():
+            away = 1 if side else chips - 1
+            arrived(side, away, 0)
+            (to_west(1, 1) if side else to_east(0, chips - 1)).start()
+            to_mate(side, away).start()
+        return do
+
+    def back(side, away):
+        def do():
+            arrived(side, away, 0)
+            to_mate(side, away).start()
+        return do
+
+    for side in (0, 1):
+        if_side(side, own_rows(side))
+    for side in (0, 1):
+        if_side(side, onward(side))
+    for side in (0, 1):
+        if_side(side, back(side, chips - 1 if side else 1))
+    for side in (0, 1):
+        if_side(side, back(side, 2))
+
+    def rest(side):
+        def do():
+            for away in range(chips):
+                arrived(side, away, 1)
+            to_east(side, 0).wait_send()
+            to_west(side, 0).wait_send()
+            (to_west(1, 1) if side else to_east(0, chips - 1)).wait_send()
+            for away in range(chips):
+                to_mate(side, away).wait_send()
+        return do
+
+    for side in (0, 1):
+        if_side(side, rest(side))
+    @pl.when(leaf < leaves - 1)
+    def _():
+        halo(0).wait_send()
+    @pl.when(leaf > 0)
+    def _():
+        halo(1).wait_send()
 
 
 def window(leaves, samples_t):
@@ -181,7 +243,13 @@
         out_shape=jax.ShapeDtypeStruct((group * count, 2 * HB * 128), samples_t.dtype),
         in_specs=[vmem],
         out_specs=vmem,
-        scratch_shapes=[pltpu.SemaphoreType.DMA((2, group))] * 2,
+        scratch_shapes=[
+            pltpu.SemaphoreType.DMA((2,)),
+            pltpu.SemaphoreType.DMA((2, 2)),
+            pltpu.SemaphoreType.DMA((2, 2)),
+            pltpu.SemaphoreType.DMA((2, group // 2)),
+            pltpu.SemaphoreType.DMA((2, group // 2, 2)),
+        ],
         compiler_params=pltpu.CompilerParams(collective_id=0, has_side_effects=True),
         cost_estimate=pl.CostEstimate(flops=0, bytes_accessed=1 << 20, transcendentals=0),
     )(samples_t)
@@ -195,13 +263,13 @@
 def product_kernel(cols, A, own, win, z, products, gram):
     leaf = lax.axis_index("leaf")
     count = own.shape[0]
-    depth = cols.shape[0]
+    depth = cols.shape[1]
     mine = pl.ds(pl.multiple_of(lax.axis_index("samp") * count, count), count)
 
     def one_row(r):
         far, near = [], []
         for k in range(NB):
-            local = cols[r, k] - leaf * depth
+            local = cols[k, r] - leaf * depth
             inside = (local >= 0) & (local < depth)
             place = jnp.clip(jnp.where(local < 0, local + HB, local - depth + HB), 0, 2 * HB - 1)
             pick = win[:, pl.ds(pl.multiple_of(place * 128, 128), 128)]
@@ -244,7 +312,7 @@
         in_specs=[pl.BlockSpec(memory_space=pltpu.SMEM), vmem, vmem, vmem],
         out_specs=[vmem] * 3,
         cost_estimate=pl.CostEstimate(flops=10**10, bytes_accessed=8 << 20, transcendentals=0),
-    )(stored_block_column, stiffness_block_row, samples_t, win)
+    )(jnp.transpose(stored_block_column), stiffness_block_row, samples_t, win)
 
 
 def levels_kernel(gram, levels, part, got, pair_send, pair_recv, all_send, all_recv):
@@ -329,8 +397,8 @@
     mine = pl.ds(pl.multiple_of(lax.axis_index("samp") * count, count), count)
     bases[...] = dot_nn(W[0, mine, :], z[...]) * math.sqrt(width)
     for k, out in enumerate((one, two, three)):
-        out[...] = dot_nt(W[k + 1], U[k, mine, :])
-    top[...] = jnp.transpose(U[3, mine, :]) * (1.0 / math.sqrt(2**LEVELS * width))
+        out[...] = dot_nt(U[k, mine, :], W[k + 1])
+    top[...] = U[3, mine, :] * (1.0 / math.sqrt(2**LEVELS * width))
 
 
 def finish(gram, levels, z, count):
@@ -339,7 +407,7 @@
     vmem = pl.BlockSpec(memory_space=pltpu.VMEM)
     return pl.pallas_call(
         finish_kernel,
-        out_shape=[jax.ShapeDtypeStruct((count, width), f32)] + [jax.ShapeDtypeStruct((order, count), f32)] * 4,
+        out_shape=[jax.ShapeDtypeStruct((count, width), f32)] + [jax.ShapeDtypeStruct((count, order), f32)] * 4,
         in_specs=[vmem] * 3,
         out_specs=[vmem] * 5,
         scratch_shapes=[pltpu.VMEM((4, order, order), f32)] * 2 + [pltpu.VMEM((8 * RS, 128), f32)] * 2,
@@ -351,7 +419,8 @@
     win = window(leaves, samples_t)
     z, products, gram = product(stiffness_block_row, stored_block_column, samples_t, win)
     levels = exchange(gram)
-    return (products,) + tuple(finish(gram, levels, z, samples_t.shape[0]))
+    bases, *transposed = finish(gram, levels, z, samples_t.shape[0])
+    return (products, bases) + tuple(jnp.transpose(t) for t in transposed)
 
 
 def solution(mesh):

time: 81.4 us -> 74 us (0.909)
  local copies, waits for them, and re-layouts: 7.73 us -> 0 us
    unnamed x5 -> x0, local copies, waits for them, and re-layouts: 7.73 us -> none
where the time goes in v3:
time: 74 us; the launch traced here: 73.8 us
  Pallas kernels  73.2 us (99%)
    pallas_call x1, Pallas kernels, exchange(): pl.pallas_call(levels_kernel, out_shape=jax.ShapeDtypeStruct((LEVELS, gro...  27.1 us
    pallas_call x1, Pallas kernels, window(): pl.pallas_call(functools.partial(window_kernel, leaves), out_shape=jax.Sh...  17.5 us
    pallas_call x1, Pallas kernels, finish(): pl.pallas_call(finish_kernel, out_shape=[jax.ShapeDtypeStruct((count, wid...  16.7 us
    pallas_call x1, Pallas kernels, product(): pl.pallas_call(product_kernel, out_shape=[jax.ShapeDtypeStruct((win.shape...  11.9 us

profile of v3, /device:TPU:1, one launch (start us, length us, event | category | flops | bytes accessed | tf_op | source)
XLA Modules:
  0.0 73.8 jit_solution(4137085552751555814)
XLA Ops:
  0.6 17.5 %shard_map.82.win = bf16[256,1024]{1,0:T(8,128)(2,1)} custom-call(bf16[32,2048]{1,0:T(8,128)(2,1)} %own.3), custom_call_target="tpu_custom_call" | custom-call | bytes 1048576 | tf_op jit(solution)/shard_map/pallas_call | solution.py:241
  18.2 11.9 %shard_map.83 = (f32[256,2048]{1,0:T(8,128)}, f32[32,2048]{1,0:T(8,128)}, f32[3,128,128]{2,1,0:T(8,128)}) custom-call(s32[8,16]{1,0:T(8,128)} %bitcast.5, bf16[16,8,128,128]{3,2,1,0:T(8,128)(2,1)} %A.1, bf16[32,2048]{1,0:T(8,128)(2,1)} %own.3, bf16[256,1024]{1,0:T(8,128)(2,1)} %shard_map.82.win), custom_call_target="tpu_custom_call" | custom-call | flops 10000000000 | bytes 8388608 | tf_op jit(solution)/shard_map/pallas_call | solution.py:305
  30.1 27.1 %shard_map.84.lv = f32[3,8,48,128]{3,2,1,0:T(8,128)} custom-call(f32[3,128,128]{2,1,0:T(8,128)} %get-tuple-element.15.gram.g0), custom_call_target="tpu_custom_call" | custom-call | bytes 1048576 | tf_op jit(solution)/shard_map/pallas_call | solution.py:371
  57.1 16.7 %shard_map.85 = (f32[32,2048]{1,0:T(8,128)}, f32[32,256]{1,0:T(8,128)}, f32[32,256]{1,0:T(8,128)}, f32[32,256]{1,0:T(8,128)}, f32[32,256]{1,0:T(8,128)}) custom-call(f32[3,128,128]{2,1,0:T(8,128)} %get-tuple-element.15.gram.g0, f32[3,8,48,128]{3,2,1,0:T(8,128)} %shard_map.84.lv, f32[256,2048]{1,0:T(8,128)} %get-tuple-element.16.z), custom_call_target="tpu_custom_call" | custom-call | flops 10000000000 | bytes 4194304 | tf_op jit(solution)/shard_map/pallas_call | solution.py:408

commit v4 on v3

--- a/solution.py
+++ b/solution.py
@@ -32,46 +32,56 @@
 def rows(i):
     return pl.ds(i, 8, stride=RS)
 
-def panel8(x, y, r0):
-    a = [[lane(x[p], r0 + q) if q >= p else None for q in range(8)] for p in range(8)]
-    for p in range(8):
-        r = lax.rsqrt(a[p][p])
-        u = [a[p][q] * r if q > p else None for q in range(8)]
-        x[p] = x[p] * r
-        y[p] = y[p] * r
-        for s in range(p + 1, 8):
-            for q in range(s, 8):
-                a[s][q] = a[s][q] - u[s] * u[q]
-            x[s] = x[s] - u[s] * x[p]
-            y[s] = y[s] - u[s] * y[p]
-    return x, y
-
-def factor(X, Y, nb, sp=32):
+def diagonal(xs, base, lo):
+    return [[lane(xs[lo + p], base + lo + q) if q >= p else None for q in range(8)] for p in range(8)]
+
+def factor(X, Y, nb, sp=16):
+    column = lax.broadcasted_iota(jnp.int32, (1, 128), 1)
     for t in range(128 // sp):
         base = t * sp
         if t:
+            solved = column < base
             for b in range(nb):
                 lhs = X[b * RS:b * RS + base, base:base + sp]
-                rhs = jnp.concatenate([X[b * RS:b * RS + base, :], Y[b * RS:b * RS + base, :], Y[(4 + b) * RS:(4 + b) * RS + base, :]], axis=1)
-                up = dot_tn(lhs, rhs)
+                left = jnp.where(solved, Y[(4 + b) * RS:(4 + b) * RS + base, :], X[b * RS:b * RS + base, :])
+                up = dot_tn(lhs, jnp.concatenate([left, Y[b * RS:b * RS + base, :]], axis=1))
                 now = X[b * RS + base:b * RS + base + sp, :] - up[:, :128]
                 X[b * RS + base:b * RS + base + sp, :] = now
                 X[(4 + b) * RS + base:(4 + b) * RS + base + sp, :] = now
-                Y[b * RS + base:b * RS + base + sp, :] -= up[:, 128:256]
-                Y[(4 + b) * RS + base:(4 + b) * RS + base + sp, :] -= up[:, 256:]
+                Y[b * RS + base:b * RS + base + sp, :] -= up[:, 128:]
+                Y[(4 + b) * RS + base:(4 + b) * RS + base + sp, :] -= jnp.where(solved, up[:, :128], 0.0)
         xs = [X[rows(base + i), :] for i in range(sp)]
         ys = [Y[rows(base + i), :] for i in range(sp)]
-        for g in range(sp // 8):
-            lo = g * 8
-            nx, ny = panel8(xs[lo:lo + 8], ys[lo:lo + 8], base + lo)
+        a = diagonal(xs, base, 0)
+        for lo in range(0, sp, 8):
+            ahead = diagonal(xs, base, lo + 8) if lo + 8 < sp else None
             for p in range(8):
-                X[rows(base + lo + p), :] = nx[p]
-                Y[rows(base + lo + p), :] = ny[p]
-            for i in range(lo + 8, sp):
+                r = lax.rsqrt(a[p][p])
+                inv = r * r
+                x = xs[lo + p] * r
+                y = ys[lo + p] * r
+                xs[lo + p], ys[lo + p] = x, y
+                X[rows(base + lo + p), :] = x
+                Y[rows(base + lo + p), :] = y
+                for s in range(p + 1, 8):
+                    u = a[p][s] * r
+                    xs[lo + s] = xs[lo + s] - u * x
+                    ys[lo + s] = ys[lo + s] - u * y
+                    for q in range(s, 8):
+                        a[s][q] = a[s][q] - (a[p][s] * a[p][q]) * inv
+                if ahead is not None:
+                    m = [lane(x, base + lo + 8 + j) for j in range(8)]
+                    for s in range(8):
+                        for q in range(s, 8):
+                            ahead[s][q] = ahead[s][q] - m[s] * m[q]
+                        xs[lo + 8 + s] = xs[lo + 8 + s] - m[s] * x
+                        ys[lo + 8 + s] = ys[lo + 8 + s] - m[s] * y
+            for i in range(lo + 16, sp):
                 for p in range(8):
-                    m = lane(nx[p], base + i)
-                    xs[i] = xs[i] - m * nx[p]
-                    ys[i] = ys[i] - m * ny[p]
+                    m = lane(xs[lo + p], base + i)
+                    xs[i] = xs[i] - m * xs[lo + p]
+                    ys[i] = ys[i] - m * ys[lo + p]
+            a = ahead
 
 def cholesky_inverse(G, U, W, X, Y, nb):
     r = lax.broadcasted_iota(jnp.int32, (128, 128), 0)
@@ -260,16 +270,26 @@
     return dot_nt_fast(jnp.concatenate(picks, axis=1), jnp.concatenate(blocks, axis=1))
 
 
-def product_kernel(cols, A, own, win, z, products, gram):
+def split3(x):
+    high = x.astype(jnp.bfloat16)
+    rest = x - high.astype(jnp.float32)
+    mid = rest.astype(jnp.bfloat16)
+    low = (rest - mid.astype(jnp.float32)).astype(jnp.bfloat16)
+    return high, mid, low
+
+
+def product_kernel(cols, A, own, win, z, products, gram, acc):
     leaf = lax.axis_index("leaf")
     count = own.shape[0]
     depth = cols.shape[1]
+    here = A.shape[0]
+    q = pl.program_id(0)
     mine = pl.ds(pl.multiple_of(lax.axis_index("samp") * count, count), count)
 
-    def one_row(r):
+    def one_row(i):
         far, near = [], []
         for k in range(NB):
-            local = cols[k, r] - leaf * depth
+            local = cols[k, q * here + i] - leaf * depth
             inside = (local >= 0) & (local < depth)
             place = jnp.clip(jnp.where(local < 0, local + HB, local - depth + HB), 0, 2 * HB - 1)
             pick = win[:, pl.ds(pl.multiple_of(place * 128, 128), 128)]
@@ -277,31 +297,42 @@
             pick = own[:, pl.ds(pl.multiple_of(jnp.clip(local, 0, depth - 1) * 128, 128), 128)]
             near.append(jnp.where(inside, pick, jnp.zeros_like(pick)))
         both = [jnp.concatenate([f, n], axis=0) for f, n in zip(far, near)]
-        out = block_row(A, both, r)
+        out = block_row(A, both, i)
         return out[:-count], out[-count:]
 
-    gram[...] = jnp.zeros_like(gram)
-
-    def step(q, carry):
-        parts = [one_row(2 * q + i) for i in range(2)]
-        pair = jnp.concatenate([p[0] for p in parts], axis=1)
-        here = pl.ds(pl.multiple_of(q * 256, 256), 256)
-        z[:, here] = pair
-        products[:, here] = jnp.concatenate([p[1] for p in parts], axis=1)
-        upper = dot_nt(pair[:128], pair)
-        gram[0] += upper[:, :128]
-        gram[1] += upper[:, 128:]
-        gram[2] += dot_nt(pair[128:], pair[128:])
-        return carry
-
-    lax.fori_loop(0, depth // 2, step, 0)
-    products[...] += z[mine, :]
+    parts = [one_row(i) for i in range(here)]
+    pair = jnp.concatenate([p[0] for p in parts], axis=1)
+    z[...] = pair
+    products[...] = jnp.concatenate([p[1] for p in parts], axis=1) + z[mine, :]
+    high, mid, low = split3(pair)
+    tops = dot_nt_fast(high, jnp.concatenate([high, mid, low], axis=0))
+    even = tops[:, :256] + dot_nt_fast(mid, mid)
+    odd = tops[:, 256:512] + tops[:, 512:]
+
+    @pl.when(q == 0)
+    def _():
+        acc[0] = even
+        acc[1] = odd
+
+    @pl.when(q > 0)
+    def _():
+        acc[0] += even
+        acc[1] += odd
+
+    @pl.when(q == pl.num_programs(0) - 1)
+    def _():
+        g = acc[0] + (acc[1] + jnp.transpose(acc[1]))
+        gram[0] = g[:128, :128]
+        gram[1] = g[:128, 128:]
+        gram[2] = g[128:, 128:]
 
 
 def product(stiffness_block_row, stored_block_column, samples_t, win):
     f32 = jnp.float32
     count, width = samples_t.shape
-    vmem = pl.BlockSpec(memory_space=pltpu.VMEM)
+    depth = stored_block_column.shape[0]
+    here = 8
+    whole = lambda shape: pl.BlockSpec(shape, lambda q: (0,) * len(shape), pipeline_mode=pl.Buffered(1))
     return pl.pallas_call(
         product_kernel,
         out_shape=[
@@ -309,8 +340,19 @@
             jax.ShapeDtypeStruct((count, width), f32),
             jax.ShapeDtypeStruct((3, 128, 128), f32),
         ],
-        in_specs=[pl.BlockSpec(memory_space=pltpu.SMEM), vmem, vmem, vmem],
-        out_specs=[vmem] * 3,
+        grid=(depth // here,),
+        in_specs=[
+            pl.BlockSpec(memory_space=pltpu.SMEM),
+            pl.BlockSpec((here,) + stiffness_block_row.shape[1:], lambda q: (q, 0, 0, 0)),
+            whole(samples_t.shape),
+            whole(win.shape),
+        ],
+        out_specs=[
+            pl.BlockSpec((win.shape[0], here * 128), lambda q: (0, q)),
+            pl.BlockSpec((count, here * 128), lambda q: (0, q)),
+            pl.BlockSpec((3, 128, 128), lambda q: (0, 0, 0)),
+        ],
+        scratch_shapes=[pltpu.VMEM((2, 256, 256), f32)],
         cost_estimate=pl.CostEstimate(flops=10**10, bytes_accessed=8 << 20, transcendentals=0),
     )(jnp.transpose(stored_block_column), stiffness_block_row, samples_t, win)
 
@@ -386,8 +428,10 @@
     )(gram)
 
 
-def finish_kernel(g0, lv, z, bases, one, two, three, top, U, W, X, Y):
+def finish_kernel(g0, lv, z_far, bases, one, two, three, top, U, W, X, Y, z, z_sem):
     count, width = bases.shape
+    load = pltpu.make_async_copy(z_far, z, z_sem)
+    load.start()
     slab = lv.shape[2] // 3
     def block(b, j):
         if b == 0:
@@ -395,6 +439,7 @@
         return jnp.concatenate([lv[b - 1, s, j * slab:(j + 1) * slab, :] for s in range(lv.shape[1])], axis=0)
     cholesky_inverse(block, U, W, X, Y, 4)
     mine = pl.ds(pl.multiple_of(lax.axis_index("samp") * count, count), count)
+    load.wait()
     bases[...] = dot_nn(W[0, mine, :], z[...]) * math.sqrt(width)
     for k, out in enumerate((one, two, three)):
         out[...] = dot_nt(U[k, mine, :], W[k + 1])
@@ -408,9 +453,9 @@
     return pl.pallas_call(
         finish_kernel,
         out_shape=[jax.ShapeDtypeStruct((count, width), f32)] + [jax.ShapeDtypeStruct((count, order), f32)] * 4,
-        in_specs=[vmem] * 3,
+        in_specs=[vmem, vmem, pl.BlockSpec(memory_space=pl.ANY)],
         out_specs=[vmem] * 5,
-        scratch_shapes=[pltpu.VMEM((4, order, order), f32)] * 2 + [pltpu.VMEM((8 * RS, 128), f32)] * 2,
+        scratch_shapes=[pltpu.VMEM((4, order, order), f32)] * 2 + [pltpu.VMEM((8 * RS, 128), f32)] * 2 + [pltpu.VMEM((order, width), f32), pltpu.SemaphoreType.DMA],
         cost_estimate=pl.CostEstimate(flops=10**10, bytes_accessed=4 << 20, transcendentals=0),
     )(gram, levels, z)
 

time: 74 us -> 68.6 us (0.927)
  Pallas kernels: 73.2 us -> 67.6 us
    pallas_call x1, Pallas kernels: 11.9 us -> 7.25 us  [product(): pl.pallas_call(product_kernel, out_shape=[jax.ShapeDtypeStruct((win.shape...]
    pallas_call x1, Pallas kernels: 16.7 us -> 15.8 us  [finish(): pl.pallas_call(finish_kernel, out_shape=[jax.ShapeDtypeStruct((count, wid...]
where the time goes in v4:
time: 68.6 us; the launch traced here: 68.4 us
  Pallas kernels  67.6 us (99%)
  between operations  0.81 us (1%)
    pallas_call x1, Pallas kernels, exchange(): pl.pallas_call(levels_kernel, out_shape=jax.ShapeDtypeStruct((LEVELS, gro...  27 us
    pallas_call x1, Pallas kernels, window(): pl.pallas_call(functools.partial(window_kernel, leaves), out_shape=jax.Sh...  17.5 us
    pallas_call x1, Pallas kernels, finish(): pl.pallas_call(finish_kernel, out_shape=[jax.ShapeDtypeStruct((count, wid...  15.8 us
    pallas_call x1, Pallas kernels, product(): pl.pallas_call(product_kernel, out_shape=[jax.ShapeDtypeStruct((win.shape...  7.25 us

profile of v4, /device:TPU:1, one launch (start us, length us, event | category | flops | bytes accessed | tf_op | source)
XLA Modules:
  0.0 68.4 jit_solution(17728712760951376923)
XLA Ops:
  0.6 17.5 %shard_map.82.win = bf16[256,1024]{1,0:T(8,128)(2,1)} custom-call(bf16[32,2048]{1,0:T(8,128)(2,1)} %own.3), custom_call_target="tpu_custom_call" | custom-call | bytes 1048576 | tf_op jit(solution)/shard_map/pallas_call | solution.py:251
  18.2 7.2 %shard_map.83 = (f32[256,2048]{1,0:T(8,128)}, f32[32,2048]{1,0:T(8,128)}, f32[3,128,128]{2,1,0:T(8,128)}) custom-call(s32[8,16]{1,0:T(8,128)} %bitcast.5, bf16[16,8,128,128]{3,2,1,0:T(8,128)(2,1)} %A.1, bf16[32,2048]{1,0:T(8,128)(2,1)} %own.3, bf16[256,1024]{1,0:T(8,128)(2,1)} %shard_map.82.win), custom_call_target="tpu_custom_call" | custom-call | flops 10000000000 | bytes 8388608 | tf_op jit(solution)/shard_map/pallas_call | solution.py:336
  25.4 27.0 %shard_map.84.lv = f32[3,8,48,128]{3,2,1,0:T(8,128)} custom-call(f32[3,128,128]{2,1,0:T(8,128)} %get-tuple-element.15.gram.g0), custom_call_target="tpu_custom_call" | custom-call | bytes 1048576 | tf_op jit(solution)/shard_map/pallas_call | solution.py:413
  52.4 15.8 %shard_map.85 = (f32[32,2048]{1,0:T(8,128)}, f32[32,256]{1,0:T(8,128)}, f32[32,256]{1,0:T(8,128)}, f32[32,256]{1,0:T(8,128)}, f32[32,256]{1,0:T(8,128)}) custom-call(f32[3,128,128]{2,1,0:T(8,128)} %get-tuple-element.15.gram.g0, f32[3,8,48,128]{3,2,1,0:T(8,128)} %shard_map.84.lv, f32[256,2048]{1,0:T(8,128)} %get-tuple-element.16.z_far), custom_call_target="tpu_custom_call" | custom-call | flops 10000000000 | bytes 4194304 | tf_op jit(solution)/shard_map/pallas_call | solution.py:453

commit v5 on v4

--- a/solution.py
+++ b/solution.py
@@ -120,7 +120,19 @@
     pl.semaphore_signal(barrier, inc=1, device_id=(there, sample), device_id_type=MESH)
 
 
-def window_kernel(leaves, own, win, halo_send, east_send, west_send, mate_send, recv):
+def split3(x):
+    high = x.astype(jnp.bfloat16)
+    rest = x - high.astype(jnp.float32)
+    mid = rest.astype(jnp.bfloat16)
+    low = (rest - mid.astype(jnp.float32)).astype(jnp.bfloat16)
+    return high, mid, low
+
+
+def gather_kernel(leaves, cols, stiff, own, z_out, near, gram, levels,
+                  A, z, win, home, acc, part, got, load_sem, z_sem,
+                  halo_send, east_send, west_send, mate_send, recv, pair_send, pair_recv, all_send, all_recv):
+    load = pltpu.make_async_copy(stiff, A, load_sem)
+    load.start()
     leaf = lax.axis_index("leaf")
     me = lax.axis_index("samp")
     group = lax.axis_size("samp")
@@ -138,19 +150,28 @@
     @pl.when(leaf < leaves - 1)
     def _():
         greet(barrier, leaf + 1, me)
-    for peer in (east, west, mate):
-        greet(barrier, leaf, peer)
+    for hop in HOPS[:-1]:
+        greet(barrier, leaf, lax.rem(me + hop, group))
+    partners = [leaf + (1 << h) - 2 * (1 << h) * lax.rem(leaf // (1 << h), 2) for h in range(LEVELS)]
+    for h in range(1, LEVELS):
+        greet(barrier, partners[h], me)
+    depth = own.shape[1] // 128
+    win[HB:HB + depth] = jnp.zeros((depth,) + win.shape[1:], win.dtype)
+    for edge in (0, HB + depth):
+        home[edge:edge + HB] = jnp.zeros((HB,) + home.shape[1:], home.dtype)
+    for j in range(depth):
+        home[HB + j] = own[:, j * 128:(j + 1) * 128]
     @pl.when(leaf == 0)
     def _():
-        win[:, :width] = jnp.zeros((win.shape[0], width), win.dtype)
+        win[:HB] = jnp.zeros((HB,) + win.shape[1:], win.dtype)
     @pl.when(leaf == leaves - 1)
     def _():
-        win[:, width:] = jnp.zeros((win.shape[0], width), win.dtype)
+        win[HB + depth:] = jnp.zeros((HB,) + win.shape[1:], win.dtype)
     neighbours = jnp.minimum(leaf, 1) + jnp.minimum(leaves - 1 - leaf, 1)
-    pl.semaphore_wait(barrier, 3 + neighbours)
+    pl.semaphore_wait(barrier, group - 1 + LEVELS - 1 + neighbours)
 
     def place(side, sample):
-        return win.at[pl.ds(pl.multiple_of(sample * count, count), count), pl.ds(side * width, width)]
+        return win.at[pl.ds(side * (HB + depth), HB), pl.ds(pl.multiple_of(sample * count, count), count), :]
 
     def send(source, side, sample, send_sem, slot, there, to):
         return pltpu.make_async_remote_copy(
@@ -159,8 +180,8 @@
         )
 
     def halo(side):
-        tail = own.at[:, pl.ds((own.shape[1] - width) * (1 - side), width)]
-        return send(tail, side, me, halo_send.at[side], (0, 0), leaf + 1 - 2 * side, me)
+        first = HB + (depth - HB) * (1 - side)
+        return send(home.at[pl.ds(first, HB)], side, me, halo_send.at[side], (0, 0), leaf + 1 - 2 * side, me)
 
     def origin(away):
         return 2 * lax.rem(chip + away, chips) + core
@@ -225,8 +246,6 @@
 
     def rest(side):
         def do():
-            for away in range(chips):
-                arrived(side, away, 1)
             to_east(side, 0).wait_send()
             to_west(side, 0).wait_send()
             (to_west(1, 1) if side else to_east(0, chips - 1)).wait_send()
@@ -234,144 +253,49 @@
                 to_mate(side, away).wait_send()
         return do
 
-    for side in (0, 1):
-        if_side(side, rest(side))
-    @pl.when(leaf < leaves - 1)
-    def _():
-        halo(0).wait_send()
-    @pl.when(leaf > 0)
-    def _():
-        halo(1).wait_send()
-
-
-def window(leaves, samples_t):
-    count = samples_t.shape[0]
-    group = 8
-    vmem = pl.BlockSpec(memory_space=pltpu.VMEM)
-    return pl.pallas_call(
-        functools.partial(window_kernel, leaves),
-        out_shape=jax.ShapeDtypeStruct((group * count, 2 * HB * 128), samples_t.dtype),
-        in_specs=[vmem],
-        out_specs=vmem,
-        scratch_shapes=[
-            pltpu.SemaphoreType.DMA((2,)),
-            pltpu.SemaphoreType.DMA((2, 2)),
-            pltpu.SemaphoreType.DMA((2, 2)),
-            pltpu.SemaphoreType.DMA((2, group // 2)),
-            pltpu.SemaphoreType.DMA((2, group // 2, 2)),
-        ],
-        compiler_params=pltpu.CompilerParams(collective_id=0, has_side_effects=True),
-        cost_estimate=pl.CostEstimate(flops=0, bytes_accessed=1 << 20, transcendentals=0),
-    )(samples_t)
-
-
-def block_row(A, picks, r):
-    blocks = [A[r, k] for k in range(NB)]
-    return dot_nt_fast(jnp.concatenate(picks, axis=1), jnp.concatenate(blocks, axis=1))
-
-
-def split3(x):
-    high = x.astype(jnp.bfloat16)
-    rest = x - high.astype(jnp.float32)
-    mid = rest.astype(jnp.bfloat16)
-    low = (rest - mid.astype(jnp.float32)).astype(jnp.bfloat16)
-    return high, mid, low
-
-
-def product_kernel(cols, A, own, win, z, products, gram, acc):
-    leaf = lax.axis_index("leaf")
-    count = own.shape[0]
-    depth = cols.shape[1]
-    here = A.shape[0]
-    q = pl.program_id(0)
-    mine = pl.ds(pl.multiple_of(lax.axis_index("samp") * count, count), count)
-
-    def one_row(i):
-        far, near = [], []
-        for k in range(NB):
-            local = cols[k, q * here + i] - leaf * depth
-            inside = (local >= 0) & (local < depth)
-            place = jnp.clip(jnp.where(local < 0, local + HB, local - depth + HB), 0, 2 * HB - 1)
-            pick = win[:, pl.ds(pl.multiple_of(place * 128, 128), 128)]
-            far.append(jnp.where(inside, jnp.zeros_like(pick), pick))
-            pick = own[:, pl.ds(pl.multiple_of(jnp.clip(local, 0, depth - 1) * 128, 128), 128)]
-            near.append(jnp.where(inside, pick, jnp.zeros_like(pick)))
-        both = [jnp.concatenate([f, n], axis=0) for f, n in zip(far, near)]
-        out = block_row(A, both, i)
-        return out[:-count], out[-count:]
-
-    parts = [one_row(i) for i in range(here)]
-    pair = jnp.concatenate([p[0] for p in parts], axis=1)
-    z[...] = pair
-    products[...] = jnp.concatenate([p[1] for p in parts], axis=1) + z[mine, :]
-    high, mid, low = split3(pair)
-    tops = dot_nt_fast(high, jnp.concatenate([high, mid, low], axis=0))
-    even = tops[:, :256] + dot_nt_fast(mid, mid)
-    odd = tops[:, 256:512] + tops[:, 512:]
-
-    @pl.when(q == 0)
-    def _():
-        acc[0] = even
-        acc[1] = odd
-
-    @pl.when(q > 0)
-    def _():
-        acc[0] += even
-        acc[1] += odd
-
-    @pl.when(q == pl.num_programs(0) - 1)
-    def _():
-        g = acc[0] + (acc[1] + jnp.transpose(acc[1]))
-        gram[0] = g[:128, :128]
-        gram[1] = g[:128, 128:]
-        gram[2] = g[128:, 128:]
-
-
-def product(stiffness_block_row, stored_block_column, samples_t, win):
-    f32 = jnp.float32
-    count, width = samples_t.shape
-    depth = stored_block_column.shape[0]
-    here = 8
-    whole = lambda shape: pl.BlockSpec(shape, lambda q: (0,) * len(shape), pipeline_mode=pl.Buffered(1))
-    return pl.pallas_call(
-        product_kernel,
-        out_shape=[
-            jax.ShapeDtypeStruct((win.shape[0], width), f32),
-            jax.ShapeDtypeStruct((count, width), f32),
-            jax.ShapeDtypeStruct((3, 128, 128), f32),
-        ],
-        grid=(depth // here,),
-        in_specs=[
-            pl.BlockSpec(memory_space=pltpu.SMEM),
-            pl.BlockSpec((here,) + stiffness_block_row.shape[1:], lambda q: (q, 0, 0, 0)),
-            whole(samples_t.shape),
-            whole(win.shape),
-        ],
-        out_specs=[
-            pl.BlockSpec((win.shape[0], here * 128), lambda q: (0, q)),
-            pl.BlockSpec((count, here * 128), lambda q: (0, q)),
-            pl.BlockSpec((3, 128, 128), lambda q: (0, 0, 0)),
-        ],
-        scratch_shapes=[pltpu.VMEM((2, 256, 256), f32)],
-        cost_estimate=pl.CostEstimate(flops=10**10, bytes_accessed=8 << 20, transcendentals=0),
-    )(jnp.transpose(stored_block_column), stiffness_block_row, samples_t, win)
-
-
-def levels_kernel(gram, levels, part, got, pair_send, pair_recv, all_send, all_recv):
-    leaf = lax.axis_index("leaf")
-    me = lax.axis_index("samp")
-    group = lax.axis_size("samp")
-    barrier = pltpu.get_barrier_semaphore()
-    partners = [leaf + (1 << h) - 2 * (1 << h) * lax.rem(leaf // (1 << h), 2) for h in range(LEVELS)]
-    for h in reversed(range(LEVELS)):
-        greet(barrier, partners[h], me)
-    for hop in HOPS[:-1]:
-        greet(barrier, leaf, lax.rem(me + hop, group))
+    def from_mate(side):
+        def do():
+            for away in range(chips):
+                arrived(side, away, 1)
+        return do
+
+    for side in (0, 1):
+        if_side(side, from_mate(side))
+    load.wait()
+    unroll = 4
+
+    def step(q, carry):
+        parts = []
+        for i in range(unroll):
+            r = q * unroll + i
+            at = [jnp.clip(cols[k, r] - (leaf * depth - HB), 0, depth + 2 * HB - 1) for k in range(NB)]
+            far = jnp.concatenate([win[j] for j in at], axis=1)
+            close = jnp.concatenate([home[j] for j in at], axis=1)
+            blocks = jnp.concatenate([A[r, k] for k in range(NB)], axis=1)
+            parts.append(dot_nt_fast(jnp.concatenate([far, close], axis=0), blocks))
+        pair = jnp.concatenate([p[:-count] for p in parts], axis=1)
+        here = pl.ds(pl.multiple_of(q * (unroll * 128), unroll * 128), unroll * 128)
+        z[:, here] = pair
+        near[:, here] = jnp.concatenate([p[-count:] for p in parts], axis=1)
+        high, mid, low = split3(pair)
+        tops = dot_nt_fast(high, jnp.concatenate([high, mid, low], axis=0))
+        acc[0] += tops[:, :256] + dot_nt_fast(mid, mid)
+        acc[1] += tops[:, 256:512] + tops[:, 512:]
+        return carry
+
+    acc[...] = jnp.zeros_like(acc)
+    lax.fori_loop(0, depth // unroll, step, 0)
+    store = pltpu.make_async_copy(z, z_out, z_sem)
+    store.start()
+    g = acc[0] + (acc[1] + jnp.transpose(acc[1]))
+    gram[0] = g[:128, :128]
+    gram[1] = g[:128, 128:]
+    gram[2] = g[128:, 128:]
+
     slab = 128 // group
     rows_here = pl.ds(pl.multiple_of(me * slab, slab), slab)
     for j in range(3):
         part[0, j * slab:(j + 1) * slab, :] = gram[j, rows_here, :]
-    pl.semaphore_wait(barrier, group - 1 + LEVELS)
 
     def trade(h):
         return pltpu.make_async_remote_copy(
@@ -403,32 +327,62 @@
         trade(h).wait_send()
         for hop in HOPS[:-1]:
             share(h, me, lax.rem(me + hop, group), hop).wait_send()
-
-
-def exchange(gram):
+    for side in (0, 1):
+        if_side(side, rest(side))
+    @pl.when(leaf < leaves - 1)
+    def _():
+        halo(0).wait_send()
+    @pl.when(leaf > 0)
+    def _():
+        halo(1).wait_send()
+    store.wait()
+
+
+def gather(leaves, stiffness_block_row, stored_block_column, samples_t):
     f32 = jnp.float32
+    count, width = samples_t.shape
+    depth = width // 128
     group = 8
+    order = group * count
     slab = 128 // group
     vmem = pl.BlockSpec(memory_space=pltpu.VMEM)
+    far = pl.BlockSpec(memory_space=pl.ANY)
+    dma = pltpu.SemaphoreType.DMA
     return pl.pallas_call(
-        levels_kernel,
-        out_shape=jax.ShapeDtypeStruct((LEVELS, group, 3 * slab, 128), f32),
-        in_specs=[vmem],
-        out_specs=vmem,
+        functools.partial(gather_kernel, leaves),
+        out_shape=[
+            jax.ShapeDtypeStruct((order, width), f32),
+            jax.ShapeDtypeStruct((count, width), f32),
+            jax.ShapeDtypeStruct((3, 128, 128), f32),
+            jax.ShapeDtypeStruct((LEVELS, group, 3 * slab, 128), f32),
+        ],
+        in_specs=[pl.BlockSpec(memory_space=pltpu.SMEM), far, vmem],
+        out_specs=[far, vmem, vmem, vmem],
         scratch_shapes=[
+            pltpu.VMEM(stiffness_block_row.shape, stiffness_block_row.dtype),
+            pltpu.VMEM((order, width), f32),
+            pltpu.VMEM((2 * HB + depth, order, 128), samples_t.dtype),
+            pltpu.VMEM((2 * HB + depth, count, 128), samples_t.dtype),
+            pltpu.VMEM((2, order, order), f32),
             pltpu.VMEM((LEVELS + 1, 3 * slab, 128), f32),
             pltpu.VMEM((LEVELS, 3 * slab, 128), f32),
-            pltpu.SemaphoreType.DMA((LEVELS,)),
-            pltpu.SemaphoreType.DMA((LEVELS,)),
-            pltpu.SemaphoreType.DMA((LEVELS, group)),
-            pltpu.SemaphoreType.DMA((LEVELS, group)),
+            dma,
+            dma,
+            dma((2,)),
+            dma((2, 2)),
+            dma((2, 2)),
+            dma((2, group // 2)),
+            dma((2, group // 2, 2)),
+            dma((LEVELS,)),
+            dma((LEVELS,)),
+            dma((LEVELS, group)),
+            dma((LEVELS, group)),
         ],
-        compiler_params=pltpu.CompilerParams(collective_id=1, has_side_effects=True),
-        cost_estimate=pl.CostEstimate(flops=0, bytes_accessed=1 << 20, transcendentals=0),
-    )(gram)
-
-
-def finish_kernel(g0, lv, z_far, bases, one, two, three, top, U, W, X, Y, z, z_sem):
+        compiler_params=pltpu.CompilerParams(collective_id=0, has_side_effects=True),
+    )(jnp.transpose(stored_block_column), stiffness_block_row, samples_t)
+
+
+def finish_kernel(g0, lv, near, z_far, products, bases, one, two, three, top, U, W, X, Y, z, z_sem):
     count, width = bases.shape
     load = pltpu.make_async_copy(z_far, z, z_sem)
     load.start()
@@ -440,31 +394,31 @@
     cholesky_inverse(block, U, W, X, Y, 4)
     mine = pl.ds(pl.multiple_of(lax.axis_index("samp") * count, count), count)
     load.wait()
+    products[...] = near[...] + z[mine, :]
     bases[...] = dot_nn(W[0, mine, :], z[...]) * math.sqrt(width)
     for k, out in enumerate((one, two, three)):
         out[...] = dot_nt(U[k, mine, :], W[k + 1])
     top[...] = U[3, mine, :] * (1.0 / math.sqrt(2**LEVELS * width))
 
 
-def finish(gram, levels, z, count):
+def finish(gram, levels, near, z):
     order, width = z.shape
+    count = near.shape[0]
     f32 = jnp.float32
     vmem = pl.BlockSpec(memory_space=pltpu.VMEM)
     return pl.pallas_call(
         finish_kernel,
-        out_shape=[jax.ShapeDtypeStruct((count, width), f32)] + [jax.ShapeDtypeStruct((count, order), f32)] * 4,
-        in_specs=[vmem, vmem, pl.BlockSpec(memory_space=pl.ANY)],
-        out_specs=[vmem] * 5,
+        out_shape=[jax.ShapeDtypeStruct((count, width), f32)] * 2 + [jax.ShapeDtypeStruct((count, order), f32)] * 4,
+        in_specs=[vmem, vmem, vmem, pl.BlockSpec(memory_space=pl.ANY)],
+        out_specs=[vmem] * 6,
         scratch_shapes=[pltpu.VMEM((4, order, order), f32)] * 2 + [pltpu.VMEM((8 * RS, 128), f32)] * 2 + [pltpu.VMEM((order, width), f32), pltpu.SemaphoreType.DMA],
         cost_estimate=pl.CostEstimate(flops=10**10, bytes_accessed=4 << 20, transcendentals=0),
-    )(gram, levels, z)
+    )(gram, levels, near, z)
 
 
 def shards(leaves, stiffness_block_row, stored_block_column, samples_t):
-    win = window(leaves, samples_t)
-    z, products, gram = product(stiffness_block_row, stored_block_column, samples_t, win)
-    levels = exchange(gram)
-    bases, *transposed = finish(gram, levels, z, samples_t.shape[0])
+    z, near, gram, levels = gather(leaves, stiffness_block_row, stored_block_column, samples_t)
+    products, bases, *transposed = finish(gram, levels, near, z)
     return (products, bases) + tuple(jnp.transpose(t) for t in transposed)
 
 

time: 68.6 us -> 62.4 us (0.910)
  Pallas kernels: 67.6 us -> 61.6 us
    pallas_call x3 -> x1, Pallas kernels: 51.8 us -> 45.8 us  [gather(): pl.pallas_call(functools.partial(gather_kernel, leaves), out_shape=[jax.S...]
where the time goes in v5:
time: 62.4 us; the launch traced here: 62.2 us
  Pallas kernels  61.6 us (99%)
  between operations  0.64 us (1%)
    pallas_call x1, Pallas kernels, gather(): pl.pallas_call(functools.partial(gather_kernel, leaves), out_shape=[jax.S...  45.8 us
    pallas_call x1, Pallas kernels, finish(): pl.pallas_call(finish_kernel, out_shape=[jax.ShapeDtypeStruct((count, wid...  15.8 us

profile of v5, /device:TPU:1, one launch (start us, length us, event | category | flops | bytes accessed | tf_op | source)
XLA Modules:
  0.0 62.2 jit_solution(5377248475912321723)
XLA Ops:
  0.6 45.8 %shard_map.82 = (f32[256,2048]{1,0:T(8,128)}, f32[32,2048]{1,0:T(8,128)}, f32[3,128,128]{2,1,0:T(8,128)}, f32[3,8,48,128]{3,2,1,0:T(8,128)}) custom-call(s32[8,16]{1,0:T(8,128)} %bitcast.5, bf16[16,8,128,128]{3,2,1,0:T(8,128)(2,1)} %stiff.1, bf16[32,2048]{1,0:T(8,128)(2,1)} %own.1), custom_call_target="tpu_custom_call" | custom-call | tf_op jit(solution)/shard_map/pallas_call | solution.py:351
  46.4 15.8 %shard_map.83 = (f32[32,2048]{1,0:T(8,128)}, f32[32,2048]{1,0:T(8,128)}, f32[32,256]{1,0:T(8,128)}, f32[32,256]{1,0:T(8,128)}, f32[32,256]{1,0:T(8,128)}, /*index=5*/f32[32,256]{1,0:T(8,128)}) custom-call(f32[3,128,128]{2,1,0:T(8,128)} %get-tuple-element.16.g0, f32[3,8,48,128]{3,2,1,0:T(8,128)} %get-tuple-element.17.lv, f32[32,2048]{1,0:T(8,128)} %get-tuple-element.18.near, ...), custom_call_target="tpu_custom_call" | custom-call | flops 10000000000 | bytes 4194304 | tf_op jit(solution)/shard_map/pallas_call | solution.py:409

commit v6 on v5

--- a/solution.py
+++ b/solution.py
@@ -11,20 +11,40 @@
 LEVELS = 3
 HOPS = (4, 5, 3, 6, 2, 7, 1, 0)
 MESH = pl.DeviceIdType.MESH
-HI = lax.Precision.HIGHEST
 RS = 136
 
+def split3(x):
+    high = x.astype(jnp.bfloat16)
+    rest = x - high.astype(jnp.float32)
+    mid = rest.astype(jnp.bfloat16)
+    low = (rest - mid.astype(jnp.float32)).astype(jnp.bfloat16)
+    return high, mid, low
+
+
+def dot_split(a, b, over_a, over_b):
+    free = 1 - over_a
+    count = a.shape[free]
+    parts = split3(a)
+    out = None
+    for k in (2, 1, 0):
+        left = parts[0] if k == 2 else jnp.concatenate(parts[:3 - k], axis=free)
+        piece = lax.dot_general(left, b[k], (((over_a,), (over_b,)), ((), ())), preferred_element_type=jnp.float32)
+        for i in reversed(range(3 - k)):
+            term = piece[i * count:(i + 1) * count]
+            out = term if out is None else out + term
+    return out
+
+
 def dot_tn(a, b):
-    return lax.dot_general(a, b, (((0,), (0,)), ((), ())), precision=HI, preferred_element_type=jnp.float32)
+    return dot_split(a, split3(b), 0, 0)
+
 
 def dot_nt(a, b):
-    return lax.dot_general(a, b, (((1,), (1,)), ((), ())), precision=HI, preferred_element_type=jnp.float32)
+    return dot_split(a, split3(b), 1, 1)
+
 
 def dot_nt_fast(a, b):
     return lax.dot_general(a, b, (((1,), (1,)), ((), ())), preferred_element_type=jnp.float32)
-
-def dot_nn(a, b):
-    return lax.dot_general(a, b, (((1,), (0,)), ((), ())), precision=HI, preferred_element_type=jnp.float32)
 
 def lane(v, j):
     return jnp.broadcast_to(v[:, j:j + 1], v.shape)
@@ -120,16 +140,8 @@
     pl.semaphore_signal(barrier, inc=1, device_id=(there, sample), device_id_type=MESH)
 
 
-def split3(x):
-    high = x.astype(jnp.bfloat16)
-    rest = x - high.astype(jnp.float32)
-    mid = rest.astype(jnp.bfloat16)
-    low = (rest - mid.astype(jnp.float32)).astype(jnp.bfloat16)
-    return high, mid, low
-
-
-def gather_kernel(leaves, cols, stiff, own, z_out, near, gram, levels,
-                  A, z, win, home, acc, part, got, load_sem, z_sem,
+def gather_kernel(leaves, cols, stiff, own, z, near, gram, levels,
+                  A, win, home, acc, part, got, load_sem,
                   halo_send, east_send, west_send, mate_send, recv, pair_send, pair_recv, all_send, all_recv):
     load = pltpu.make_async_copy(stiff, A, load_sem)
     load.start()
@@ -285,8 +297,6 @@
 
     acc[...] = jnp.zeros_like(acc)
     lax.fori_loop(0, depth // unroll, step, 0)
-    store = pltpu.make_async_copy(z, z_out, z_sem)
-    store.start()
     g = acc[0] + (acc[1] + jnp.transpose(acc[1]))
     gram[0] = g[:128, :128]
     gram[1] = g[:128, 128:]
@@ -335,7 +345,6 @@
     @pl.when(leaf > 0)
     def _():
         halo(1).wait_send()
-    store.wait()
 
 
 def gather(leaves, stiffness_block_row, stored_block_column, samples_t):
@@ -346,7 +355,6 @@
     order = group * count
     slab = 128 // group
     vmem = pl.BlockSpec(memory_space=pltpu.VMEM)
-    far = pl.BlockSpec(memory_space=pl.ANY)
     dma = pltpu.SemaphoreType.DMA
     return pl.pallas_call(
         functools.partial(gather_kernel, leaves),
@@ -356,17 +364,15 @@
             jax.ShapeDtypeStruct((3, 128, 128), f32),
             jax.ShapeDtypeStruct((LEVELS, group, 3 * slab, 128), f32),
         ],
-        in_specs=[pl.BlockSpec(memory_space=pltpu.SMEM), far, vmem],
-        out_specs=[far, vmem, vmem, vmem],
+        in_specs=[pl.BlockSpec(memory_space=pltpu.SMEM), pl.BlockSpec(memory_space=pltpu.HBM), vmem],
+        out_specs=[vmem] * 4,
         scratch_shapes=[
             pltpu.VMEM(stiffness_block_row.shape, stiffness_block_row.dtype),
-            pltpu.VMEM((order, width), f32),
             pltpu.VMEM((2 * HB + depth, order, 128), samples_t.dtype),
             pltpu.VMEM((2 * HB + depth, count, 128), samples_t.dtype),
             pltpu.VMEM((2, order, order), f32),
             pltpu.VMEM((LEVELS + 1, 3 * slab, 128), f32),
             pltpu.VMEM((LEVELS, 3 * slab, 128), f32),
-            dma,
             dma,
             dma((2,)),
             dma((2, 2)),
@@ -378,14 +384,12 @@
             dma((LEVELS, group)),
             dma((LEVELS, group)),
         ],
-        compiler_params=pltpu.CompilerParams(collective_id=0, has_side_effects=True),
+        compiler_params=pltpu.CompilerParams(collective_id=0, has_side_effects=True, vmem_limit_bytes=52000000),
     )(jnp.transpose(stored_block_column), stiffness_block_row, samples_t)
 
 
-def finish_kernel(g0, lv, near, z_far, products, bases, one, two, three, top, U, W, X, Y, z, z_sem):
+def finish_kernel(g0, lv, near, z, products, bases, one, two, three, top, U, W, X, Y):
     count, width = bases.shape
-    load = pltpu.make_async_copy(z_far, z, z_sem)
-    load.start()
     slab = lv.shape[2] // 3
     def block(b, j):
         if b == 0:
@@ -393,9 +397,8 @@
         return jnp.concatenate([lv[b - 1, s, j * slab:(j + 1) * slab, :] for s in range(lv.shape[1])], axis=0)
     cholesky_inverse(block, U, W, X, Y, 4)
     mine = pl.ds(pl.multiple_of(lax.axis_index("samp") * count, count), count)
-    load.wait()
     products[...] = near[...] + z[mine, :]
-    bases[...] = dot_nn(W[0, mine, :], z[...]) * math.sqrt(width)
+    bases[...] = dot_split(W[0, mine, :], split3(z[...]), 1, 0) * math.sqrt(width)
     for k, out in enumerate((one, two, three)):
         out[...] = dot_nt(U[k, mine, :], W[k + 1])
     top[...] = U[3, mine, :] * (1.0 / math.sqrt(2**LEVELS * width))
@@ -409,9 +412,10 @@
     return pl.pallas_call(
         finish_kernel,
         out_shape=[jax.ShapeDtypeStruct((count, width), f32)] * 2 + [jax.ShapeDtypeStruct((count, order), f32)] * 4,
-        in_specs=[vmem, vmem, vmem, pl.BlockSpec(memory_space=pl.ANY)],
+        in_specs=[vmem] * 4,
         out_specs=[vmem] * 6,
-        scratch_shapes=[pltpu.VMEM((4, order, order), f32)] * 2 + [pltpu.VMEM((8 * RS, 128), f32)] * 2 + [pltpu.VMEM((order, width), f32), pltpu.SemaphoreType.DMA],
+        scratch_shapes=[pltpu.VMEM((4, order, order), f32)] * 2 + [pltpu.VMEM((8 * RS, 128), f32)] * 2,
+        compiler_params=pltpu.CompilerParams(vmem_limit_bytes=52000000),
         cost_estimate=pl.CostEstimate(flops=10**10, bytes_accessed=4 << 20, transcendentals=0),
     )(gram, levels, near, z)
 

time: 62.4 us -> 60.5 us (0.970)
  Pallas kernels: 61.6 us -> 58.1 us
  local copies, waits for them, and re-layouts: 0 us -> 1.58 us
    pallas_call x1, Pallas kernels: 15.8 us -> 13.6 us  [finish(): pl.pallas_call(finish_kernel, out_shape=[jax.ShapeDtypeStruct((count, wid...]
    unnamed x0 -> x4, local copies, waits for them, and re-layouts: none -> 1.58 us
    pallas_call x1, Pallas kernels: 45.8 us -> 44.5 us  [gather(): pl.pallas_call(functools.partial(gather_kernel, leaves), out_shape=[jax.S...]
where the time goes in v6:
time: 60.5 us; the launch traced here: 60.3 us
  Pallas kernels  58.1 us (96%)
  local copies, waits for them, and re-layouts  1.58 us (3%)
  between operations  0.65 us (1%)
    pallas_call x1, Pallas kernels, gather(): pl.pallas_call(functools.partial(gather_kernel, leaves), out_shape=[jax.S...  44.5 us
    pallas_call x1, Pallas kernels, finish(): pl.pallas_call(finish_kernel, out_shape=[jax.ShapeDtypeStruct((count, wid...  13.6 us
    unnamed x4, local copies, waits for them, and re-layouts  1.58 us

profile of v6, /device:TPU:1, one launch (start us, length us, event | category | flops | bytes accessed | tf_op | source)
XLA Modules:
  0.0 60.3 jit_solution(15869364560971306566)
XLA Ops:
  0.6 0.0 copy-start
  0.6 0.9 %copy-done = bf16[32,2048]{1,0:T(8,128)(2,1)S(1)} copy-done((bf16[32,2048]{1,0:T(8,128)(2,1)S(1)}, bf16[32,2048]{1,0:T(8,128)(2,1)}, u32[]{:S(2)}) %copy-start) | copy-done | bytes 131096
  1.5 0.0 copy-start.1
  1.5 0.7 %copy-done.1 = s32[16,8]{0,1:T(8,128)S(1)} copy-done((s32[16,8]{0,1:T(8,128)S(1)}, s32[16,8]{0,1:T(8,128)}, u32[]{:S(2)}) %copy-start.1) | copy-done | bytes 536
  2.2 44.5 %shard_map.82 = (f32[256,2048]{1,0:T(8,128)S(1)}, f32[32,2048]{1,0:T(8,128)S(1)}, f32[3,128,128]{2,1,0:T(8,128)S(1)}, f32[3,8,48,128]{3,2,1,0:T(8,128)S(1)}) custom-call(s32[8,16]{1,0:T(8,128)S(1)} %bitcast.5, bf16[16,8,128,128]{3,2,1,0:T(8,128)(2,1)} %stiff.1, bf16[32,2048]{1,0:T(8,128)(2,1)S(1)} %copy-done), custom_call_target="tpu_custom_call" | custom-call | tf_op jit(solution)/shard_map/pallas_call | solution.py:359
  46.7 13.6 %shard_map.83 = (f32[32,2048]{1,0:T(8,128)}, f32[32,2048]{1,0:T(8,128)}, f32[32,256]{1,0:T(8,128)}, f32[32,256]{1,0:T(8,128)}, f32[32,256]{1,0:T(8,128)}, /*index=5*/f32[32,256]{1,0:T(8,128)}) custom-call(f32[3,128,128]{2,1,0:T(8,128)S(1)} %get-tuple-element.16.g0, f32[3,8,48,128]{3,2,1,0:T(8,128)S(1)} %get-tuple-element.17.lv, ...), custom_call_target="tpu_custom_call" | custom-call | flops 10000000000 | bytes 4194304 | tf_op jit(solution)/shard_map/pallas_call | solution.py:412
Async XLA Ops:
  0.6 0.9 %copy-start = (bf16[32,2048]{1,0:T(8,128)(2,1)S(1)}, bf16[32,2048]{1,0:T(8,128)(2,1)}, u32[]{:S(2)}) copy-start(bf16[32,2048]{1,0:T(8,128)(2,1)} %own.1) | copy-start | bytes 393220
  1.5 0.7 %copy-start.1 = (s32[16,8]{0,1:T(8,128)S(1)}, s32[16,8]{0,1:T(8,128)}, u32[]{:S(2)}) copy-start(s32[16,8]{0,1:T(8,128)} %param.4) | copy-start | bytes 1540

commit v7 on v6

--- a/solution.py
+++ b/solution.py
@@ -140,9 +140,11 @@
     pl.semaphore_signal(barrier, inc=1, device_id=(there, sample), device_id_type=MESH)
 
 
-def gather_kernel(leaves, cols, stiff, own, z, near, gram, levels,
-                  A, win, home, acc, part, got, load_sem,
+def gather_kernel(leaves, cols, stiff, samples, z, near, gram, levels,
+                  A, own, own_sem, win, home, acc, part, got, load_sem,
                   halo_send, east_send, west_send, mate_send, recv, pair_send, pair_recv, all_send, all_recv):
+    fetch = pltpu.make_async_copy(samples, own, own_sem)
+    fetch.start()
     load = pltpu.make_async_copy(stiff, A, load_sem)
     load.start()
     leaf = lax.axis_index("leaf")
@@ -171,6 +173,7 @@
     win[HB:HB + depth] = jnp.zeros((depth,) + win.shape[1:], win.dtype)
     for edge in (0, HB + depth):
         home[edge:edge + HB] = jnp.zeros((HB,) + home.shape[1:], home.dtype)
+    fetch.wait()
     for j in range(depth):
         home[HB + j] = own[:, j * 128:(j + 1) * 128]
     @pl.when(leaf == 0)
@@ -364,10 +367,12 @@
             jax.ShapeDtypeStruct((3, 128, 128), f32),
             jax.ShapeDtypeStruct((LEVELS, group, 3 * slab, 128), f32),
         ],
-        in_specs=[pl.BlockSpec(memory_space=pltpu.SMEM), pl.BlockSpec(memory_space=pltpu.HBM), vmem],
+        in_specs=[pl.BlockSpec(memory_space=pltpu.SMEM), pl.BlockSpec(memory_space=pltpu.HBM), pl.BlockSpec(memory_space=pltpu.HBM)],
         out_specs=[vmem] * 4,
         scratch_shapes=[
             pltpu.VMEM(stiffness_block_row.shape, stiffness_block_row.dtype),
+            pltpu.VMEM(samples_t.shape, samples_t.dtype),
+            dma,
             pltpu.VMEM((2 * HB + depth, order, 128), samples_t.dtype),
             pltpu.VMEM((2 * HB + depth, count, 128), samples_t.dtype),
             pltpu.VMEM((2, order, order), f32),
@@ -384,8 +389,8 @@
             dma((LEVELS, group)),
             dma((LEVELS, group)),
         ],
-        compiler_params=pltpu.CompilerParams(collective_id=0, has_side_effects=True, vmem_limit_bytes=52000000),
-    )(jnp.transpose(stored_block_column), stiffness_block_row, samples_t)
+        compiler_params=pltpu.CompilerParams(collective_id=0, has_side_effects=True, vmem_limit_bytes=52500000),
+    )(jnp.transpose(stored_block_column), stiffness_block_row, pltpu.with_memory_space_constraint(samples_t, pltpu.HBM))
 
 
 def finish_kernel(g0, lv, near, z, products, bases, one, two, three, top, U, W, X, Y):
@@ -415,7 +420,7 @@
         in_specs=[vmem] * 4,
         out_specs=[vmem] * 6,
         scratch_shapes=[pltpu.VMEM((4, order, order), f32)] * 2 + [pltpu.VMEM((8 * RS, 128), f32)] * 2,
-        compiler_params=pltpu.CompilerParams(vmem_limit_bytes=52000000),
+        compiler_params=pltpu.CompilerParams(vmem_limit_bytes=52500000),
         cost_estimate=pl.CostEstimate(flops=10**10, bytes_accessed=4 << 20, transcendentals=0),
     )(gram, levels, near, z)
 

time: 60.5 us -> 59.6 us (0.985)
  local copies, waits for them, and re-layouts: 1.58 us -> 0.68 us
    unnamed x4 -> x2, local copies, waits for them, and re-layouts: 1.58 us -> 0.68 us
where the time goes in v7:
time: 59.6 us; the launch traced here: 59.4 us
  Pallas kernels  58.1 us (97%)
  local copies, waits for them, and re-layouts  0.68 us (1%)
  between operations  0.65 us (1%)
    pallas_call x1, Pallas kernels, gather(): pl.pallas_call(functools.partial(gather_kernel, leaves), out_shape=[jax.S...  44.5 us
    pallas_call x1, Pallas kernels, finish(): pl.pallas_call(finish_kernel, out_shape=[jax.ShapeDtypeStruct((count, wid...  13.6 us

profile of v7, /device:TPU:1, one launch (start us, length us, event | category | flops | bytes accessed | tf_op | source)
XLA Modules:
  0.0 59.4 jit_solution(10176645125362525015)
XLA Ops:
  0.6 0.0 copy-start
  0.6 0.7 %copy-done = s32[16,8]{0,1:T(8,128)S(1)} copy-done((s32[16,8]{0,1:T(8,128)S(1)}, s32[16,8]{0,1:T(8,128)}, u32[]{:S(2)}) %copy-start) | copy-done | bytes 536
  1.3 44.5 %shard_map.82 = (f32[256,2048]{1,0:T(8,128)S(1)}, f32[32,2048]{1,0:T(8,128)S(1)}, f32[3,128,128]{2,1,0:T(8,128)S(1)}, f32[3,8,48,128]{3,2,1,0:T(8,128)S(1)}) custom-call(s32[8,16]{1,0:T(8,128)S(1)} %bitcast.5, bf16[16,8,128,128]{3,2,1,0:T(8,128)(2,1)} %stiff.1, bf16[32,2048]{1,0:T(8,128)(2,1)} %samples.1), custom_call_target="tpu_custom_call" | custom-call | tf_op jit(solution)/shard_map/pallas_call | solution.py:362
  45.8 13.6 %shard_map.83 = (f32[32,2048]{1,0:T(8,128)}, f32[32,2048]{1,0:T(8,128)}, f32[32,256]{1,0:T(8,128)}, f32[32,256]{1,0:T(8,128)}, f32[32,256]{1,0:T(8,128)}, /*index=5*/f32[32,256]{1,0:T(8,128)}) custom-call(f32[3,128,128]{2,1,0:T(8,128)S(1)} %get-tuple-element.16.g0, f32[3,8,48,128]{3,2,1,0:T(8,128)S(1)} %get-tuple-element.17.lv, ...), custom_call_target="tpu_custom_call" | custom-call | flops 10000000000 | bytes 4194304 | tf_op jit(solution)/shard_map/pallas_call | solution.py:417
Async XLA Ops:
  0.6 0.7 %copy-start = (s32[16,8]{0,1:T(8,128)S(1)}, s32[16,8]{0,1:T(8,128)}, u32[]{:S(2)}) copy-start(s32[16,8]{0,1:T(8,128)} %param.4) | copy-start | bytes 1540
